TPU v7x, 256 devices: a whole 4x4x8 slice. The times are simulated.
256 devices in a mesh: cells: 32 (over z, y), mem: 8 (over x, core).
Axes of the slice: x: 4, y: 4, z: 8, core: 2. Of those that a mesh axis runs over, the one named last changes fastest.
Arguments:
- background_copies: bfloat16 [512, 262144], P('mem', 'cells')
- measuring_span_leading_cell: int32 [131072], P(('cells', 'mem')), may hold values from 0 to 1023, as said below
- measuring_kernel_coefficients: bfloat16 [131072, 4], P(('cells', 'mem')), may hold values from -3 to 3
- measured_readings: float32 [131072], P(('cells', 'mem')), may hold values from -18 to 18
- measured_error_precision: float32 [131072], P(('cells', 'mem')), may hold values from 0.00078125 to 0.0078125
Outputs:
- analysis: float32 [512, 262144], P(None, ('cells', 'mem'))
Inputs may be any that keep to these rules, and one draw needn't show every extreme that they name: `measuring_span_leading_cell`: in every block of 512 observations the first one's window starts at one of the last 3 cells of the block and the second one's at the block's last cell.
All inputs are finite; a program needn't handle non-finite values.
Results may differ from a plain program's by a relative error of at most 0.0014.
The roundings to bfloat16 on the way count: a program that leaves them out, or rounds other values in their place, can miss the bound.
Values may be sent and summed in bfloat16 or wider, within the bound.
A program may use at most 64 MiB of HBM per device.

v0:
```python
import math

import jax
import jax.numpy as jnp
from jax import lax
from jax.sharding import PartitionSpec as P


def passed_along(value, axis, steps):
    count = lax.axis_size(axis)
    pairs = [(source, (source + steps) % count) for source in range(count)]
    return lax.ppermute(value, axis, pairs)


def operator_table(offsets, weights, first_column, columns):
    position = lax.broadcasted_iota(jnp.int32, (offsets.shape[0], columns), 1) + first_column
    table = jnp.zeros((offsets.shape[0], columns), jnp.bfloat16)
    for window_step in range(weights.shape[1]):
        table = table + jnp.where(
            position == offsets[:, None] + window_step,
            weights[:, window_step : window_step + 1],
            jnp.zeros((), jnp.bfloat16),
        )
    return table


def precise_dot(left, right):
    return jnp.dot(left, right, precision=lax.Precision.HIGHEST)


def block_cholesky(square):
    extent = square.shape[0]
    positions = jnp.arange(extent, dtype=jnp.int32)

    def column_step(column, lower):
        row_now = lax.dynamic_slice_in_dim(lower, column, 1, 0)[0]
        source = lax.dynamic_slice_in_dim(square, column, 1, 1)[:, 0]
        remains = source - precise_dot(lower, row_now)
        pivot = jnp.sqrt(lax.dynamic_slice_in_dim(remains, column, 1, 0)[0])
        fresh = jnp.where(positions >= column, remains / pivot, jnp.zeros_like(remains))
        return lax.dynamic_update_slice_in_dim(lower, fresh[:, None], column, 1)

    return lax.fori_loop(0, extent, column_step, jnp.zeros_like(square))


def block_invert_lower(lower):
    extent = lower.shape[0]
    positions = jnp.arange(extent, dtype=jnp.int32)

    def row_step(row_index, inverse):
        lower_row = lax.dynamic_slice_in_dim(lower, row_index, 1, 0)[0]
        pivot = lax.dynamic_slice_in_dim(lower_row, row_index, 1, 0)[0]
        unit_row = (positions == row_index).astype(lower.dtype)
        fresh = (unit_row - precise_dot(lower_row, inverse)) / pivot
        return lax.dynamic_update_slice_in_dim(inverse, fresh[None, :], row_index, 0)

    return lax.fori_loop(0, extent, row_step, jnp.zeros_like(lower))


def factor_and_invert(system):
    extent = system.shape[0]
    width = min(128, extent)
    count = extent // width
    lower = jnp.zeros_like(system)
    diagonal_inverses = []
    for block_index in range(count):
        begin = block_index * width
        panel = system[begin:, begin : begin + width]
        if block_index > 0:
            panel = panel - precise_dot(
                lower[begin:, :begin], lower[begin : begin + width, :begin].T
            )
        diagonal_factor = block_cholesky(panel[:width])
        diagonal_inverse = block_invert_lower(diagonal_factor)
        diagonal_inverses.append(diagonal_inverse)
        lower = lower.at[begin : begin + width, begin : begin + width].set(diagonal_factor)
        if begin + width < extent:
            lower = lower.at[begin + width :, begin : begin + width].set(
                precise_dot(panel[width:], diagonal_inverse.T)
            )
    inverse = jnp.zeros_like(system)
    for block_index in range(count):
        begin = block_index * width
        inverse = inverse.at[begin : begin + width, begin : begin + width].set(
            diagonal_inverses[block_index]
        )
        if block_index > 0:
            earlier = precise_dot(lower[begin : begin + width, :begin], inverse[:begin, :begin])
            inverse = inverse.at[begin : begin + width, :begin].set(
                -precise_dot(diagonal_inverses[block_index], earlier)
            )
    return inverse


def local(
    background_copies,
    measuring_span_leading_cell,
    measuring_kernel_coefficients,
    measured_readings,
    measured_error_precision,
):
    predicted_copies = background_copies.shape[0] * lax.axis_size("mem")
    sea_grid_piece = lax.all_to_all(
        background_copies, "mem", split_axis=1, concat_axis=0, tiled=True
    )
    cells_here = sea_grid_piece.shape[1]
    reach = measuring_kernel_coefficients.shape[1]
    edge_cells = jnp.transpose(sea_grid_piece[:, : reach - 1])
    outside_extension = passed_along(edge_cells, ("cells", "mem"), -1)
    predicted_centroid = jnp.sum(sea_grid_piece, axis=0, dtype=jnp.float32) / predicted_copies
    copy_anomalies = (sea_grid_piece.astype(jnp.float32) - predicted_centroid[None, :]).astype(
        jnp.bfloat16
    )
    outside_centroid = jnp.sum(outside_extension, axis=1, dtype=jnp.float32) / predicted_copies
    beyond_anomaly = (outside_extension.astype(jnp.float32) - outside_centroid[:, None]).astype(
        jnp.bfloat16
    )
    primary_lookup = operator_table(
        measuring_span_leading_cell, measuring_kernel_coefficients, 0, cells_here
    )
    rim_table = operator_table(
        measuring_span_leading_cell, measuring_kernel_coefficients, cells_here, reach - 1
    )
    projected = lax.dot_general(
        primary_lookup, copy_anomalies, (((1,), (1,)), ((), ())), preferred_element_type=jnp.float32
    )
    projected = projected + jnp.dot(rim_table, beyond_anomaly, preferred_element_type=jnp.float32)
    observed_mean = jnp.dot(
        primary_lookup.astype(jnp.float32), predicted_centroid, precision=lax.Precision.HIGHEST
    )
    observed_mean = observed_mean + jnp.dot(
        rim_table.astype(jnp.float32), outside_centroid, precision=lax.Precision.HIGHEST
    )
    root = jnp.sqrt(measured_error_precision)
    weighted = (root[:, None] * projected).astype(jnp.bfloat16)
    innovation = (root * (measured_readings - observed_mean)).astype(jnp.bfloat16)
    gram_part = lax.dot_general(
        weighted, weighted, (((0,), (0,)), ((), ())), preferred_element_type=jnp.float32
    )
    pull_part = lax.dot_general(
        innovation, weighted, (((0,), (0,)), ((), ())), preferred_element_type=jnp.float32
    )
    inner_product_matrix, pull = lax.psum((gram_part, pull_part), ("cells", "mem"))
    linear_equations = inner_product_matrix + (predicted_copies - 1.0) * jnp.eye(
        predicted_copies, dtype=jnp.float32
    )
    lower_inverse = factor_and_invert(linear_equations)
    middle = precise_dot(lower_inverse, pull)
    stencil_displacement = precise_dot(lower_inverse.T, middle)
    scatter_square_root = math.sqrt(predicted_copies - 1.0)
    blend_matrix = (scatter_square_root * lower_inverse.T + stencil_displacement[:, None]).astype(
        jnp.bfloat16
    )
    return predicted_centroid[None, :] + lax.dot_general(
        blend_matrix, copy_anomalies, (((0,), (0,)), ((), ())), preferred_element_type=jnp.float32
    )


def solution(mesh):
    in_specs = (
        P("mem", "cells"),
        P(("cells", "mem")),
        P(("cells", "mem"), None),
        P(("cells", "mem")),
        P(("cells", "mem")),
    )
    out_specs = P(None, ("cells", "mem"))
    return jax.shard_map(local, mesh=mesh, in_specs=in_specs, out_specs=out_specs, check_vma=False)
```

profile of v0, /device:TPU:1, one launch (start us, length us, event | category | flops | bytes accessed | tf_op | source)
XLA Modules:
  0.0 2290.0 jit_solution(1323346990532241943)
XLA Ops:
  6.5 2.3 copy.17
  8.9 6.7 all-to-all-start
  15.6 15.0 all-to-all-done
  30.7 0.9 collective-permute-start
  31.8 1.4 fusion.76
  33.3 2.0 fusion.82
  35.5 1.0 fusion.106
  36.6 1.0 fusion.65
  37.6 1.4 fusion.115
  39.2 84.1 %psum.15 = f32[512]{0:T(512)S(1)} all-reduce(f32[512]{0:T(512)S(1)} %bitcast.262), channel_id=1, replica_groups=mesh['cells'=32,'mem'=8] {'cells','mem'}, use_global_device_ids=true, to_apply=%region_19.20 | all-reduce | flops 512 | bytes 4096 | tf_op jit(solution)/shard_map/psum | solution.py:143
  123.4 174.0 %all-reduce.4.cloned.1.call-done = f32[512,512]{1,0:T(8,128)} async-done(((f32[512,512]{1,0:T(8,128)}), f32[512,512]{1,0:T(8,128)}) %all-reduce.4.cloned.1.call-update) | async-done | bytes 1048592 | tf_op jit(solution)/shard_map/psum | solution.py:143
  297.4 1.3 select_add_fusion
  298.9 257.4 %while.138 = (s32[]{:T(128)}, f32[128,128]{1,0:T(8,128)S(1)}, f32[128,128]{0,1:T(8,128)S(1)}, s32[]{:T(128)}, s32[]{:T(128)}) while((s32[]{:T(128)}, f32[128,128]{1,0:T(8,128)S(1)}, f32[128,128]{0,1:T(8,128)S(1)}, s32[]{:T(128)}, s32[]{:T(128)}) %tuple.324), condition=%wide.region_4.5_spmd.clone, body=%wide.region_3.4_spmd.clone.sunk | while | flops 197122 | bytes 71261 | solution.py:43
  556.4 184.3 %while.139 = (s32[]{:T(128)}, f32[128,128]{1,0:T(8,128)S(1)}, f32[128,128]{1,0:T(8,128)S(1)}, s32[]{:T(128)}, s32[]{:T(128)}, /*index=5*/s32[]{:T(128)}) while((s32[]{:T(128)}, f32[128,128]{1,0:T(8,128)S(1)}, f32[128,128]{1,0:T(8,128)S(1)}, s32[]{:T(128)}, s32[]{:T(128)}, /*index=5*/s32[]{:T(128)}) %tuple.327), condition=%wide.region_6.7_spmd.clone, body=%wide.region_5.6_spmd.clone.sunk | while | flops 197123 | bytes 69221 | solution.py:57
  742.1 361.4 %while.140 = (s32[]{:T(128)}, f32[128,128]{1,0:T(8,128)S(1)}, f32[128,128]{0,1:T(8,128)}, s32[]{:T(128)}, s32[]{:T(128)}) while((s32[]{:T(128)}, f32[128,128]{1,0:T(8,128)S(1)}, f32[128,128]{0,1:T(8,128)}, s32[]{:T(128)}, s32[]{:T(128)}) %tuple.330), condition=%wide.region_8.9_spmd.clone, body=%wide.region_7.8_spmd.clone.sunk | while | flops 197122 | bytes 71261 | solution.py:43
  744.9 0.9 fusion.180
  747.7 0.9 fusion.180
  750.5 0.9 fusion.180
  756.2 0.9 fusion.180
  759.0 0.9 fusion.180
  761.8 0.9 fusion.180
  764.6 0.9 fusion.180
  767.5 0.9 fusion.180
  770.3 0.9 fusion.180
  773.1 0.9 fusion.180
  1103.6 184.3 %while.141 = (s32[]{:T(128)}, f32[128,128]{1,0:T(8,128)S(1)}, f32[128,128]{1,0:T(8,128)S(1)}, s32[]{:T(128)}, s32[]{:T(128)}, /*index=5*/s32[]{:T(128)}) while((s32[]{:T(128)}, f32[128,128]{1,0:T(8,128)S(1)}, f32[128,128]{1,0:T(8,128)S(1)}, s32[]{:T(128)}, s32[]{:T(128)}, /*index=5*/s32[]{:T(128)}) %tuple.333), condition=%wide.region_10.11_spmd.clone, body=%wide.region_9.10_spmd.clone.sunk | while | flops 197123 | bytes 69221 | solution.py:57
  1289.2 361.4 %while.142 = (s32[]{:T(128)}, f32[128,128]{1,0:T(8,128)S(1)}, f32[128,128]{0,1:T(8,128)}, s32[]{:T(128)}, s32[]{:T(128)}) while((s32[]{:T(128)}, f32[128,128]{1,0:T(8,128)S(1)}, f32[128,128]{0,1:T(8,128)}, s32[]{:T(128)}, s32[]{:T(128)}) %tuple.336), condition=%wide.region_12.13_spmd.clone, body=%wide.region_11.12_spmd.clone.sunk | while | flops 197122 | bytes 71261 | solution.py:43
  1650.7 184.3 %while.143 = (s32[]{:T(128)}, f32[128,128]{1,0:T(8,128)S(1)}, f32[128,128]{1,0:T(8,128)S(1)}, s32[]{:T(128)}, s32[]{:T(128)}, /*index=5*/s32[]{:T(128)}) while((s32[]{:T(128)}, f32[128,128]{1,0:T(8,128)S(1)}, f32[128,128]{1,0:T(8,128)S(1)}, s32[]{:T(128)}, s32[]{:T(128)}, /*index=5*/s32[]{:T(128)}) %tuple.339), condition=%wide.region_14.15_spmd.clone, body=%wide.region_13.14_spmd.clone.sunk | while | flops 197123 | bytes 69221 | solution.py:57
  1835.7 257.4 %while.144 = (s32[]{:T(128)}, f32[128,128]{1,0:T(8,128)S(1)}, f32[128,128]{0,1:T(8,128)S(1)}, s32[]{:T(128)}, s32[]{:T(128)}) while((s32[]{:T(128)}, f32[128,128]{1,0:T(8,128)S(1)}, f32[128,128]{0,1:T(8,128)S(1)}, s32[]{:T(128)}, s32[]{:T(128)}) %tuple.342), condition=%wide.region_16.17_spmd.clone, body=%wide.region_15.16_spmd.clone.sunk | while | flops 197122 | bytes 71261 | solution.py:43
  2093.1 184.3 %while.145 = (s32[]{:T(128)}, f32[128,128]{1,0:T(8,128)S(1)}, f32[128,128]{1,0:T(8,128)S(1)}, s32[]{:T(128)}, s32[]{:T(128)}, /*index=5*/s32[]{:T(128)}) while((s32[]{:T(128)}, f32[128,128]{1,0:T(8,128)S(1)}, f32[128,128]{1,0:T(8,128)S(1)}, s32[]{:T(128)}, s32[]{:T(128)}, /*index=5*/s32[]{:T(128)}) %tuple.345), condition=%wide.region_18.19_spmd.clone, body=%wide.region_17.18_spmd.clone.sunk | while | flops 197123 | bytes 69221 | solution.py:57
  2279.4 1.0 convolution_bitcast_fusion.8
  2281.0 2.1 convolution_add_fusion
  (4143 shorter events, 1579.2 us)
Async XLA Ops:
  6.5 9.0 copy-start
  6.5 9.1 copy-start.3
  8.9 21.8 all-to-all-start
  15.6 281.8 %all-reduce.4.cloned.1.call-start = ((), (), s32[]{:S(2)}) async-start(), calls=%async_computation.1 | async-start | bytes 2097152 | tf_op jit(solution)/shard_map/psum | solution.py:143
  30.7 4.6 collective-permute-start
  33.3 3.2 copy-start.1
  33.3 3.2 copy-start.2
Sparse Core Ops, SparseCore 0:
  39.2 258.1 all-reduce.3
where the time goes:
time: 2320 us; the launch traced here: 2290 us
  local copies, waits for them, and re-layouts  909 us (39%)
  matrix products  687 us (30%)
  loops' own time  394 us (17%)
  waiting for transfers between devices  189 us (8%)
  blocking collectives  84.1 us (4%)
    dot_general x1038, matrix products, precise_dot(): return jnp.dot(left, right, precision=lax.Precision.HIGHEST)  678 us
    another operation x4, loops' own time, block_cholesky(): return lax.fori_loop(0, extent, column_step, jnp.zeros_like(square))  382 us
    dynamic_slice x512, local copies, waits for them, and re-layouts, column_step(): pivot = jnp.sqrt(lax.dynamic_slice_in_dim(remains, column, 1, 0)[0])  346 us
    dynamic_slice x512, local copies, waits for them, and re-layouts, row_step(): pivot = lax.dynamic_slice_in_dim(lower_row, row_index, 1, 0)[0]  301 us
    dynamic_update_slice x512, local copies, waits for them, and re-layouts, column_step(): return lax.dynamic_update_slice_in_dim(lower, fresh[:, None], column, 1)  184 us
    psum x1, waiting for transfers between devices, local(): lax.psum((gram_part, pull_part), ('cells', 'mem'))  174 us
    psum x1, blocking collectives, local(): lax.psum((gram_part, pull_part), ('cells', 'mem'))  84.1 us
    broadcast_in_dim x512, local copies, waits for them, and re-layouts, column_step(): return lax.dynamic_update_slice_in_dim(lower, fresh[:, None], column, 1)  57.9 us

commit v1 on v0

v1 whole, which is shorter than its diff:
```python
import functools
import math

import jax
import jax.numpy as jnp
from jax import lax
from jax.experimental import pallas as pl
from jax.experimental.pallas import tpu as pltpu
from jax.sharding import PartitionSpec as P

F32 = jnp.float32
N_Y = 4
ROWS, LANES = 8, 128
MESH = pl.DeviceIdType.MESH


def passed_along(value, axis, steps):
    count = lax.axis_size(axis)
    pairs = [(source, (source + steps) % count) for source in range(count)]
    return lax.ppermute(value, axis, pairs)


def operator_table(offsets, weights, first_column, columns):
    position = lax.broadcasted_iota(jnp.int32, (offsets.shape[0], columns), 1) + first_column
    table = jnp.zeros((offsets.shape[0], columns), jnp.bfloat16)
    for window_step in range(weights.shape[1]):
        table = table + jnp.where(
            position == offsets[:, None] + window_step,
            weights[:, window_step : window_step + 1],
            jnp.zeros((), jnp.bfloat16),
        )
    return table


def total_kernel(n, n_mem, n_y, n_z, gram_ref, pull_ref, total_ref, pulled_ref,
                 share, mem_in, y_out, y_in, z_in,
                 mem_send, mem_recv, y_send, y_recv, z_send, z_recv, yg_send, yg_recv, mg_send, mg_recv):
    cell, mem = lax.axis_index("cells"), lax.axis_index("mem")
    y, z = lax.rem(cell, n_y), cell // n_y
    piece = share.shape[1] - ROWS
    part = piece // n_y

    def mem_peer(step):
        return (cell, lax.rem(mem + step, n_mem))

    def y_peer(step):
        return (z * n_y + lax.rem(y + step, n_y), mem)

    def z_peer(step):
        return (lax.rem(z + step, n_z) * n_y + y, mem)

    peers = (
        [mem_peer(s) for s in range(1, n_mem)]
        + [y_peer(s) for s in range(1, n_y)]
        + [z_peer(s) for s in range(1, n_z)]
    )
    barrier = pltpu.get_barrier_semaphore()
    for peer in peers:
        pl.semaphore_signal(barrier, inc=1, device_id=peer, device_id_type=MESH)

    place = 0
    for lane_block in range(n // LANES):
        begin = lane_block * LANES
        for row in range(begin, n, ROWS):
            share[place // piece, place % piece : place % piece + ROWS, :] = gram_ref[row : row + ROWS, begin : begin + LANES]
            place += ROWS
    for s in range(n_mem):
        share[s, piece : piece + ROWS, :] = pull_ref[...]
    pl.semaphore_wait(barrier, len(peers))

    copies = []
    for step in range(1, n_mem):
        peer = mem_peer(step)
        copies.append(
            pltpu.make_async_remote_copy(
                src_ref=share.at[peer[1]], dst_ref=mem_in.at[step - 1], send_sem=mem_send.at[step - 1],
                recv_sem=mem_recv.at[step - 1], device_id=peer, device_id_type=MESH,
            )
        )
    for copy in copies:
        copy.start()
    for copy in copies:
        copy.wait_recv()
    summed = share[mem]
    for step in range(n_mem - 1):
        summed = summed + mem_in[step]
    for s in range(n_y):
        y_out[s, :part, :] = summed[s * part : (s + 1) * part]
        y_out[s, part:, :] = summed[piece:]
    pending = copies

    copies = []
    for step in range(1, n_y):
        peer = y_peer(step)
        copies.append(
            pltpu.make_async_remote_copy(
                src_ref=y_out.at[lax.rem(y + step, n_y)], dst_ref=y_in.at[step - 1], send_sem=y_send.at[step - 1],
                recv_sem=y_recv.at[step - 1], device_id=peer, device_id_type=MESH,
            )
        )
    for copy in copies:
        copy.start()
    for copy in copies:
        copy.wait_recv()
    summed = y_out[y]
    for step in range(n_y - 1):
        summed = summed + y_in[step]
    z_in[z] = summed
    pending = pending + copies

    copies = []
    for step in range(1, n_z):
        copies.append(
            pltpu.make_async_remote_copy(
                src_ref=z_in.at[z], dst_ref=z_in.at[z], send_sem=z_send.at[step - 1],
                recv_sem=z_recv.at[step - 1], device_id=z_peer(step), device_id_type=MESH,
            )
        )
    for copy in copies:
        copy.start()
    for copy in copies:
        copy.wait_recv()
    summed = z_in[0]
    for s in range(1, n_z):
        summed = summed + z_in[s]
    pulled_ref[...] = summed[part:]
    own = pl.ds(pl.multiple_of(y * part, ROWS), part)
    total_ref[mem, own, :] = summed[:part]
    pending = pending + copies

    copies = []
    for step in range(1, n_y):
        copies.append(
            pltpu.make_async_remote_copy(
                src_ref=total_ref.at[mem, own], dst_ref=total_ref.at[mem, own], send_sem=yg_send.at[step - 1],
                recv_sem=yg_recv.at[step - 1], device_id=y_peer(step), device_id_type=MESH,
            )
        )
    for copy in copies:
        copy.start()
    for copy in copies:
        copy.wait_recv()
    pending = pending + copies
    copies = []
    for step in range(1, n_mem):
        copies.append(
            pltpu.make_async_remote_copy(
                src_ref=total_ref.at[mem], dst_ref=total_ref.at[mem], send_sem=mg_send.at[step - 1],
                recv_sem=mg_recv.at[step - 1], device_id=mem_peer(step), device_id_type=MESH,
            )
        )
    for copy in copies:
        copy.start()
    for copy in copies:
        copy.wait_recv()
    for copy in pending + copies:
        copy.wait_send()


def totals(gram_part, pull_tile, n_y, n_z):
    n = gram_part.shape[0]
    n_mem = lax.axis_size("mem")
    blocks = n // LANES
    packed = LANES * LANES * blocks * (blocks + 1) // 2 // LANES
    piece = packed // n_mem
    dma = pltpu.SemaphoreType.DMA
    part = piece // n_y
    return pl.pallas_call(
        functools.partial(total_kernel, n, n_mem, n_y, n_z),
        out_shape=(
            jax.ShapeDtypeStruct((n_mem, piece, LANES), F32),
            jax.ShapeDtypeStruct((ROWS, LANES), F32),
        ),
        in_specs=[pl.BlockSpec(memory_space=pltpu.VMEM)] * 2,
        out_specs=(pl.BlockSpec(memory_space=pltpu.VMEM),) * 2,
        scratch_shapes=[
            pltpu.VMEM((n_mem, piece + ROWS, LANES), F32),
            pltpu.VMEM((n_mem - 1, piece + ROWS, LANES), F32),
            pltpu.VMEM((n_y, part + ROWS, LANES), F32),
            pltpu.VMEM((n_y - 1, part + ROWS, LANES), F32),
            pltpu.VMEM((n_z, part + ROWS, LANES), F32),
            dma((n_mem - 1,)), dma((n_mem - 1,)), dma((n_y - 1,)), dma((n_y - 1,)), dma((n_z - 1,)), dma((n_z - 1,)),
            dma((n_y - 1,)), dma((n_y - 1,)), dma((n_mem - 1,)), dma((n_mem - 1,)),
        ],
        compiler_params=pltpu.CompilerParams(collective_id=0, has_side_effects=True),
        name="totals",
    )(gram_part, pull_tile)


def precise_dot(left, right, contract=((1,), (0,))):
    return lax.dot_general(
        left, right, (contract, ((), ())), precision=lax.Precision.HIGHEST, preferred_element_type=F32
    )


def inverse_factor_rows(tiles, group):
    tiles = list(tiles)
    extent = tiles[0].shape[1]
    lane = lax.broadcasted_iota(jnp.int32, (ROWS, extent), 1)
    sublane = lax.broadcasted_iota(jnp.int32, (ROWS, extent), 0)

    def spread(value):
        return jnp.broadcast_to(value, (ROWS, extent))

    for first in range(0, extent, group):
        home, top = first // ROWS, first % ROWS
        own = tiles[home]
        columns = [
            [spread(tile[:, first + a : first + a + 1]) for tile in tiles[home:]] for a in range(group)
        ]
        pivots = {
            (b, a): spread(columns[a][0][top + b : top + b + 1, :]) for a in range(group) for b in range(a, group)
        }
        member = (lane >= first) & (lane < first + group)
        rows = [
            jnp.where(member, jnp.where(lane == first + a, 1.0, 0.0), spread(own[top + a : top + a + 1, :]))
            for a in range(group)
        ]
        for a in range(group):
            scale = lax.rsqrt(pivots[(a, a)])
            rows[a] = rows[a] * scale
            columns[a] = [column * scale for column in columns[a]]
            below = {b: pivots[(b, a)] * scale for b in range(a + 1, group)}
            for b in range(a + 1, group):
                for c in range(a + 1, b + 1):
                    pivots[(b, c)] = pivots[(b, c)] - below[b] * below[c]
                rows[b] = rows[b] - below[b] * rows[a]
                columns[b] = [right - left * below[b] for right, left in zip(columns[b], columns[a])]
        for index in range(home, len(tiles)):
            if index == home and group == ROWS:
                fresh = own
            else:
                fresh = jnp.where(member, 0.0, tiles[index])
                for a in range(group):
                    fresh = fresh - columns[a][index - home] * rows[a]
            if index == home:
                fresh = jnp.where(sublane < top, own, fresh)
                for a in range(group):
                    fresh = jnp.where(sublane == top + a, rows[a], fresh)
            tiles[index] = fresh
    return tiles


def mixing_kernel(n, width, group, packed_ref, pull_ref, out_ref, work):
    shape = (width, width)
    row = lax.broadcasted_iota(jnp.int32, shape, 0)
    column = lax.broadcasted_iota(jnp.int32, shape, 1)
    unit = jnp.where(row == column, 1.0, 0.0)
    place = 0
    for begin in range(0, n, width):
        work[begin:n, begin : begin + width] = packed_ref[place : place + n - begin, :]
        place += n - begin
        index = begin // width
        work[n : n + 1, begin : begin + width] = pull_ref[index : index + 1, :]
    work[n + 1 :, :] = jnp.zeros((ROWS - 1, n), F32)
    for begin in range(0, n, width):
        end = begin + width
        block = work[begin:end, begin:end] + (n - 1.0) * unit
        tiles = inverse_factor_rows([block[i : i + ROWS] for i in range(0, width, ROWS)], group)
        inverse = jnp.where(column <= row, jnp.concatenate(tiles, axis=0), 0.0)
        below = precise_dot(work[end:, begin:end], inverse, ((1,), (1,)))
        if begin > 0:
            work[begin:end, :begin] = precise_dot(inverse, work[begin:end, :begin])
        work[begin:end, begin:end] = inverse
        work[end:, begin:end] = jnp.zeros((n + ROWS - end, width), F32)
        work[end:, :end] = work[end:, :end] - precise_dot(below, work[begin:end, :end])
        if end < n:
            work[end:, end:] = work[end:, end:] - precise_dot(below, below[: n - end], ((1,), (1,)))
    whole = (n, n)
    lower = lax.broadcasted_iota(jnp.int32, whole, 1) <= lax.broadcasted_iota(jnp.int32, whole, 0)
    scaled = jnp.where(lower, work[:n, :] * math.sqrt(n - 1.0), 0.0)
    out_ref[...] = (scaled - work[n : n + 1, :]).astype(jnp.bfloat16)


def mixing_rows(packed, pull_tile, n):
    return pl.pallas_call(
        functools.partial(mixing_kernel, n, LANES, ROWS),
        out_shape=jax.ShapeDtypeStruct((n, n), jnp.bfloat16),
        in_specs=[pl.BlockSpec(memory_space=pltpu.VMEM)] * 2,
        out_specs=pl.BlockSpec(memory_space=pltpu.VMEM),
        scratch_shapes=[pltpu.VMEM((n + ROWS, n), F32)],
        compiler_params=pltpu.CompilerParams(vmem_limit_bytes=24 << 20),
        name="mixing",
    )(packed, pull_tile)


def local(
    background_copies,
    measuring_span_leading_cell,
    measuring_kernel_coefficients,
    measured_readings,
    measured_error_precision,
):
    predicted_copies = background_copies.shape[0] * lax.axis_size("mem")
    sea_grid_piece = lax.all_to_all(
        background_copies, "mem", split_axis=1, concat_axis=0, tiled=True
    )
    cells_here = sea_grid_piece.shape[1]
    reach = measuring_kernel_coefficients.shape[1]
    edge_cells = jnp.transpose(sea_grid_piece[:, : reach - 1])
    outside_extension = passed_along(edge_cells, ("cells", "mem"), -1)
    predicted_centroid = jnp.sum(sea_grid_piece, axis=0, dtype=jnp.float32) / predicted_copies
    copy_anomalies = (sea_grid_piece.astype(jnp.float32) - predicted_centroid[None, :]).astype(
        jnp.bfloat16
    )
    outside_centroid = jnp.sum(outside_extension, axis=1, dtype=jnp.float32) / predicted_copies
    beyond_anomaly = (outside_extension.astype(jnp.float32) - outside_centroid[:, None]).astype(
        jnp.bfloat16
    )
    primary_lookup = operator_table(
        measuring_span_leading_cell, measuring_kernel_coefficients, 0, cells_here
    )
    rim_table = operator_table(
        measuring_span_leading_cell, measuring_kernel_coefficients, cells_here, reach - 1
    )
    projected = lax.dot_general(
        primary_lookup, copy_anomalies, (((1,), (1,)), ((), ())), preferred_element_type=jnp.float32
    )
    projected = projected + jnp.dot(rim_table, beyond_anomaly, preferred_element_type=jnp.float32)
    observed_mean = jnp.dot(
        primary_lookup.astype(jnp.float32), predicted_centroid, precision=lax.Precision.HIGHEST
    )
    observed_mean = observed_mean + jnp.dot(
        rim_table.astype(jnp.float32), outside_centroid, precision=lax.Precision.HIGHEST
    )
    root = jnp.sqrt(measured_error_precision)
    weighted = (root[:, None] * projected).astype(jnp.bfloat16)
    innovation = (root * (measured_readings - observed_mean)).astype(jnp.bfloat16)
    gram_part = lax.dot_general(
        weighted, weighted, (((0,), (0,)), ((), ())), preferred_element_type=jnp.float32
    )
    pull_part = lax.dot_general(
        innovation, weighted, (((0,), (0,)), ((), ())), preferred_element_type=jnp.float32
    )
    blocks = predicted_copies // LANES
    pull_tile = jnp.concatenate(
        [pull_part.reshape(blocks, LANES), jnp.zeros((ROWS - blocks, LANES), F32)], axis=0
    )
    n_z = lax.axis_size("cells") // N_Y
    total, pulled = totals(gram_part, pull_tile, N_Y, n_z)
    mixing_transposed = mixing_rows(total.reshape(-1, LANES), pulled, predicted_copies)
    return predicted_centroid[None, :] + lax.dot_general(
        mixing_transposed, copy_anomalies, (((1,), (0,)), ((), ())), preferred_element_type=jnp.float32
    )


def solution(mesh):
    in_specs = (
        P("mem", "cells"),
        P(("cells", "mem")),
        P(("cells", "mem"), None),
        P(("cells", "mem")),
        P(("cells", "mem")),
    )
    out_specs = P(None, ("cells", "mem"))
    return jax.shard_map(local, mesh=mesh, in_specs=in_specs, out_specs=out_specs, check_vma=False)
```

time: 2320 us -> 105 us (0.05); the launches traced: 2290 us -> 105 us
  local copies, waits for them, and re-layouts: 909 us -> 4.8 us
  matrix products: 687 us -> 9.36 us
  loops' own time: 394 us -> 0 us
  waiting for transfers between devices: 189 us -> 15.1 us
  blocking collectives: 84.1 us -> 0 us
  Pallas kernels: 0 us -> 67.5 us
    dot_general x1039 -> x1, matrix products: 680 us -> 2.06 us  [local(): lax.dot_general(mixing_transposed, copy_anomalies, (((1,), (0,)), ((), ()...]
    dynamic_slice x1024 -> x0, local copies, waits for them, and re-layouts: 648 us -> none  [the longest x512 346 us: column_step(): pivot = jnp.sqrt(lax.dynamic_slice_in_dim(remains, column, 1, 0)[0])]
    another operation x8 -> x0, loops' own time: 394 us -> none  [the longest x4 382 us: block_cholesky(): return lax.fori_loop(0, extent, column_step, jnp.zeros_like(square))]
    dynamic_update_slice x1024 -> x0, local copies, waits for them, and re-layouts: 200 us -> none  [the longest x512 184 us: column_step(): return lax.dynamic_update_slice_in_dim(lower, fresh[:, None], column, 1)]
    psum x1 -> x0, waiting for transfers between devices: 174 us -> none  [local(): lax.psum((gram_part, pull_part), ('cells', 'mem'))]
    psum x1 -> x0, blocking collectives: 84.1 us -> none  [local(): lax.psum((gram_part, pull_part), ('cells', 'mem'))]
    pallas_call x0 -> x2, Pallas kernels: none -> 67.5 us  [the longest x1 44.1 us: totals(): pl.pallas_call(functools.partial(total_kernel, n, n_mem, n_y, n_z), out_s...]
    broadcast_in_dim x512 -> x0, local copies, waits for them, and re-layouts: 57.9 us -> none  [column_step(): return lax.dynamic_update_slice_in_dim(lower, fresh[:, None], column, 1)]
where the time goes in v1:
time: 105 us
  Pallas kernels  67.5 us (64%)
  waiting for transfers between devices  15.1 us (14%)
  matrix products  9.36 us (9%)
  starting transfers between devices  7.65 us (7%)
  local copies, waits for them, and re-layouts  4.8 us (5%)
    pallas_call x1, Pallas kernels, totals(): pl.pallas_call(functools.partial(total_kernel, n, n_mem, n_y, n_z), out_s...  44.1 us
    pallas_call x1, Pallas kernels, mixing_rows(): pl.pallas_call(functools.partial(mixing_kernel, n, LANES, ROWS), out_shap...  23.4 us
    all_to_all x1, waiting for transfers between devices, local(): lax.all_to_all(background_copies, 'mem', split_axis=1, concat_axis=0, til...  15.1 us
    all_to_all x1, starting transfers between devices, local(): lax.all_to_all(background_copies, 'mem', split_axis=1, concat_axis=0, til...  6.7 us
    all_to_all x1, local copies, waits for them, and re-layouts, local(): lax.all_to_all(background_copies, 'mem', split_axis=1, concat_axis=0, til...  2.31 us
  transfers between devices with their start and end apart: 2, of which 1 were waited for; matrix products, arithmetic and copies ran while one was open for 3% of the time, Pallas kernels for 0%

profile of v1, /device:TPU:1, one launch (start us, length us, event | category | flops | bytes accessed | tf_op | source)
XLA Modules:
  0.0 104.8 jit_solution(1580111596876613768)
XLA Ops:
  0.0 0.0 copy-start.2
  0.0 0.0 copy-start.5
  0.0 2.3 %copy.9 = bf16[8,8,8,1024]{3,2,0,1:T(8,128)(2,1)} copy(bf16[8,8,8,1024]{3,2,1,0:T(8,128)(2,1)} %bitcast.30) | data formatting | bytes 2097152 | tf_op jit(solution)/shard_map/all_to_all | solution.py:295
  2.3 6.7 %all-to-all-start = ((bf16[64,8,1024]{2,0,1:T(8,128)(2,1)}), bf16[64,8,1024]{2,0,1:T(8,128)(2,1)S(1)}, u32[]{:S(2)}, u32[]{:S(2)}) async-start(bf16[64,8,1024]{2,0,1:T(8,128)(2,1)} %bitcast.25), calls=%async_computation | async-start | bytes 2097152 | tf_op jit(solution)/shard_map/all_to_all | solution.py:295
  9.0 0.0 copy-done.2
  9.1 0.0 copy-done.5
  9.1 15.1 %all-to-all-done = bf16[64,8,1024]{2,0,1:T(8,128)(2,1)S(1)} async-done(((bf16[64,8,1024]{2,0,1:T(8,128)(2,1)}), bf16[64,8,1024]{2,0,1:T(8,128)(2,1)S(1)}, u32[]{:S(2)}, u32[]{:S(2)}) %all-to-all-start) | async-done | bytes 1048608 | tf_op jit(solution)/shard_map/all_to_all | solution.py:295
  24.1 0.2 convert_reduce_fusion
  24.4 0.9 collective-permute-start
  25.3 1.4 %fusion.9 = f32[512,512]{1,0:T(8,128)S(1)} fusion(bf16[512,1024]{1,0:T(8,128)(2,1)S(1)} %bitcast.28, f32[1024]{0:T(1024)S(1)} %broadcast_multiply_fusion, s32[512]{0:T(512)S(1)} %get-tuple-element.17, s32[512]{0:T(512)S(1)} %get-tuple-element.16, s32[512]{0:T(512)S(1)} %get-tuple-element.15, s32[512]{0:T(512)S(1)} %copy-done.5, ...), kind=kOutput, calls=%fused_computation.18 | convolution fusion | flops 546832384 | bytes 2113536 | tf_op jit(solution)/shard_map/dot_general | solution.py:316
  26.7 0.0 copy-start.3
  26.8 0.0 copy-start.4
  26.8 2.0 %fusion.10 = f32[1,512]{1,0:T(1,128)S(1)} fusion(f32[1024,1]{0,1:T(1,128)S(1)} %bitcast.32, s32[512]{0:T(512)S(1)} %get-tuple-element.17, s32[512]{0:T(512)S(1)} %get-tuple-element.16, s32[512]{0:T(512)S(1)} %get-tuple-element.15, s32[512]{0:T(512)S(1)} %copy-done.5, bf16[512]{0:T(512)(128)(2,1)S(1)} %get-tuple-element.11, ...), kind=kOutput, calls=%fused_computation.19 | convolution fusion | flops 14680064 | bytes 18432 | tf_op jit(solution)/shard_map/dot_general | solution.py:320
  28.8 0.0 collective-permute-done
  28.8 0.1 convert_reduce_fusion.1
  28.9 1.0 fusion.19
  30.0 0.0 copy-done.3
  30.0 0.0 copy-done.4
  30.1 1.2 %fusion.5 = bf16[512,512]{1,0:T(8,128)(2,1)S(1)} fusion(f32[512,512]{1,0:T(8,128)S(1)} %fusion.9, f32[512]{0:T(512)S(1)} %get-tuple-element.14, bf16[3,512]{0,1:T(8,128)(2,1)S(1)} %collective-permute-done, f32[3]{0:T(128)S(1)} %broadcast_multiply_fusion.1, s32[3]{0:T(128)S(1)} %iota_add_fusion, s32[512]{0:T(512)S(1)} %get-tuple-element.17, ...), kind=kOutput, calls=%fused_computation.13 | convolution fusion | flops 2380800 | bytes 1590296 | tf_op jit(solution)/shard_map/dot_general | solution.py:319
  31.3 1.4 %fusion.27.gram_ref = f32[512,512]{1,0:T(8,128)} fusion(bf16[512,512]{1,0:T(8,128)(2,1)S(1)} %fusion.5), kind=kOutput, calls=%fused_computation.49 | convolution fusion | flops 268435456 | bytes 1572864 | tf_op jit(solution)/shard_map/dot_general | solution.py:329
  32.7 0.2 fusion.28
  32.9 0.6 concatenate.3.pull_ref
  33.5 44.1 %totals.1 = (f32[8,160,128]{2,1,0:T(8,128)}, f32[8,128]{1,0:T(8,128)}) custom-call(f32[512,512]{1,0:T(8,128)} %fusion.27.gram_ref, f32[8,128]{1,0:T(8,128)} %concatenate.3.pull_ref), custom_call_target="tpu_custom_call" | custom-call | tf_op jit(solution)/shard_map/totals/pallas_call | solution.py:168
  77.6 0.0 copy-start
  77.6 1.1 %copy-done = f32[8,160,128]{2,1,0:T(8,128)S(1)} copy-done((f32[8,160,128]{2,1,0:T(8,128)S(1)}, f32[8,160,128]{2,1,0:T(8,128)}, u32[]{:S(2)}) %copy-start) | copy-done | bytes 655384
  78.7 0.0 copy-start.1
  78.7 0.7 copy-done.1
  79.4 23.4 %mixing.1 = bf16[512,512]{1,0:T(8,128)(2,1)S(1)} custom-call(f32[1280,128]{1,0:T(8,128)S(1)} %bitcast.26, f32[8,128]{1,0:T(8,128)S(1)} %copy-done.1), custom_call_target="tpu_custom_call" | custom-call | tf_op jit(solution)/shard_map/mixing/pallas_call | solution.py:276
  102.8 2.1 %convolution_add_fusion = f32[512,1024]{1,0:T(8,128)} fusion(bf16[512,512]{1,0:T(8,128)(2,1)S(1)} %mixing.1, f32[1024]{0:T(1024)S(1)} %broadcast_multiply_fusion, bf16[512,1024]{1,0:T(8,128)(2,1)S(1)} %bitcast.29), kind=kOutput, calls=%fused_computation.10 | convolution fusion | flops 538968064 | bytes 3674112 | tf_op jit(solution)/shard_map/dot_general | solution.py:342
  (8 shorter events, 0.1 us)
Async XLA Ops:
  0.0 9.0 %copy-start.2 = (bf16[512,4]{0,1:T(4,128)(2,1)S(1)}, bf16[512,4]{0,1:T(4,128)(2,1)}, u32[]{:S(2)}) copy-start(bf16[512,4]{0,1:T(4,128)(2,1)} %param.7) | copy-start | bytes 12292
  0.0 9.1 %copy-start.5 = (s32[512]{0:T(512)S(1)}, s32[512]{0:T(512)}, u32[]{:S(2)}) copy-start(s32[512]{0:T(512)} %param.6) | copy-start | bytes 6148
  2.3 21.8 %all-to-all-start = ((bf16[64,8,1024]{2,0,1:T(8,128)(2,1)}), bf16[64,8,1024]{2,0,1:T(8,128)(2,1)S(1)}, u32[]{:S(2)}, u32[]{:S(2)}) async-start(bf16[64,8,1024]{2,0,1:T(8,128)(2,1)} %bitcast.25), calls=%async_computation | async-start | bytes 2097152 | tf_op jit(solution)/shard_map/all_to_all | solution.py:295
  24.4 4.5 %collective-permute-start = (bf16[3,512]{0,1:T(8,128)(2,1)S(1)}, bf16[3,512]{0,1:T(8,128)(2,1)S(1)}, u32[]{:S(2)}, u32[]{:S(2)}) collective-permute-start(bf16[3,512]{0,1:T(8,128)(2,1)S(1)} %slice_bitcast_fusion), channel_id=1, source_target_pairs={{0,255},{1,0},{2,1},{3,2},{4,3},{5,4},{6,5},{7,6},{8,7},{9,8},{10,... | collective-permute-start | bytes 9224 | tf_op jit(solution)/shard_map/ppermute | solution.py:20
  26.7 3.2 %copy-start.3 = (f32[512]{0:T(512)S(1)}, f32[512]{0:T(512)}, u32[]{:S(2)}) copy-start(f32[512]{0:T(512)} %param.8) | copy-start | bytes 6148
  26.8 3.2 %copy-start.4 = (f32[512]{0:T(512)S(1)}, f32[512]{0:T(512)}, u32[]{:S(2)}) copy-start(f32[512]{0:T(512)} %param.9) | copy-start | bytes 6148
  77.6 1.1 %copy-start = (f32[8,160,128]{2,1,0:T(8,128)S(1)}, f32[8,160,128]{2,1,0:T(8,128)}, u32[]{:S(2)}) copy-start(f32[8,160,128]{2,1,0:T(8,128)} %get-tuple-element.7) | copy-start | bytes 1966084
  78.7 0.7 copy-start.1

commit v2 on v1

v2 whole, which is shorter than its diff:
```python
import functools
import math

import jax
import jax.numpy as jnp
from jax import lax
from jax.experimental import pallas as pl
from jax.experimental.pallas import tpu as pltpu
from jax.sharding import PartitionSpec as P

F32 = jnp.float32
N_Y = 4
ROWS, LANES = 8, 128
MESH = pl.DeviceIdType.MESH


def front_kernel(n_mem, n_y, n_z, field_ref, start_ref, weight_ref, reading_ref, precision_ref,
                 total_ref, pulled_ref, anomaly_ref, mean_ref,
                 state, spread_out, table, weighted, a_out, a_in, b_out, b_in, ay_out, ay_in, bm_out, bm_in, az, bz,
                 own_sem, edge_send, edge_recv, x_send, x_recv,
                 a_sem, b_sem, ay_sem, bm_sem, az_sem, bz_sem, ag_sem, bg_sem, ah_sem, bh_sem):
    cell, mem = lax.axis_index("cells"), lax.axis_index("mem")
    n_cells = n_y * n_z
    y, z = lax.rem(cell, n_y), cell // n_y
    members = field_ref.shape[0]
    n = members * n_mem
    here = anomaly_ref.shape[1]
    wide = state.shape[1]
    edge = wide - here
    last = n_mem - 1

    def mem_peer(step):
        return (cell, lax.rem(mem + step, n_mem))

    def y_peer(step):
        return (z * n_y + lax.rem(y + step, n_y), mem)

    def z_peer(step):
        return (lax.rem(z + step, n_z) * n_y + y, mem)

    def signal(peer):
        pl.semaphore_signal(barrier, inc=1, device_id=peer, device_id_type=MESH)

    barrier = pltpu.get_barrier_semaphore()
    for step in range(1, n_mem):
        signal(mem_peer(step))
    for step in range(1, n_y):
        signal(y_peer(step))
    for step in range(1, n_z):
        signal(z_peer(step))

    @pl.when(mem == last)
    def _():
        for source in range(n_mem):
            signal((lax.rem(cell + 1, n_cells), source))

    pl.semaphore_wait(barrier, n_mem + n_y + n_z - 2)

    rows_here = pl.ds(pl.multiple_of(mem * members, members), members)

    def slab_copy(step, width):
        target = lax.rem(mem + step, n_mem)
        return pltpu.make_async_remote_copy(
            src_ref=field_ref.at[:, pl.ds(pl.multiple_of(target * here, here), width)],
            dst_ref=state.at[rows_here, pl.ds(0, width)],
            send_sem=x_send.at[step - 1], recv_sem=x_recv.at[step - 1],
            device_id=mem_peer(step), device_id_type=MESH,
        )

    def arrival(step, width):
        source = lax.rem(mem + n_mem - step, n_mem)
        rows = pl.ds(pl.multiple_of(source * members, members), members)
        return pltpu.make_async_remote_copy(
            src_ref=field_ref.at[:, pl.ds(0, width)], dst_ref=state.at[rows, pl.ds(0, width)],
            send_sem=x_send.at[step - 1], recv_sem=x_recv.at[step - 1],
            device_id=mem_peer(step), device_id_type=MESH,
        )

    def own_copy(width):
        return pltpu.make_async_copy(
            field_ref.at[:, pl.ds(pl.multiple_of(mem * here, here), width)],
            state.at[rows_here, pl.ds(0, width)], own_sem,
        )

    def edge_copy(source):
        rows = pl.ds(pl.multiple_of(source * members, members), members)
        return pltpu.make_async_remote_copy(
            src_ref=field_ref.at[:, pl.ds(0, edge)], dst_ref=state.at[rows, pl.ds(here, edge)],
            send_sem=edge_send, recv_sem=edge_recv.at[source],
            device_id=(lax.rem(cell + n_cells - 1, n_cells), last), device_id_type=MESH,
        )

    for step in range(1, n_mem):
        target = lax.rem(mem + step, n_mem)

        @pl.when(target != last)
        def _(step=step):
            slab_copy(step, wide).start()

        @pl.when(target == last)
        def _(step=step):
            slab_copy(step, here).start()

    edge_copy(mem).start()

    @pl.when(mem != last)
    def _():
        own_copy(wide).start()

    @pl.when(mem == last)
    def _():
        own_copy(here).start()

    start = start_ref[...]
    taps = [weight_ref[j : j + 1, :].astype(F32) for j in range(weight_ref.shape[0])]
    chunk = 64

    @pl.loop(0, wide // chunk)
    def _(index):
        first = pl.multiple_of(index * chunk, chunk)
        ahead = lax.broadcasted_iota(jnp.int32, (chunk, start.shape[1]), 0) + first - start
        block = jnp.zeros(ahead.shape, F32)
        for j, tap in enumerate(taps):
            block = jnp.where(ahead == j, tap, block)
        table[pl.ds(first, chunk), :] = block.astype(jnp.bfloat16)

    @pl.when(mem != last)
    def _():
        own_copy(wide).wait()
        for step in range(1, n_mem):
            arrival(step, wide).wait_recv()

    @pl.when(mem == last)
    def _():
        own_copy(here).wait()
        for step in range(1, n_mem):
            arrival(step, here).wait_recv()
        for source in range(n_mem):
            edge_copy(source).wait_recv()

    step_rows = 64

    def add_rows(index, total):
        first = pl.multiple_of(index * step_rows, step_rows)
        return total + jnp.sum(state[pl.ds(first, step_rows), :].astype(F32).reshape(step_rows // ROWS, ROWS, wide), axis=0)

    sums = lax.fori_loop(0, n // step_rows, add_rows, jnp.zeros((ROWS, wide), F32))
    mean = jnp.sum(sums, axis=0, keepdims=True) / n
    mean_ref[...] = mean[:, :here]

    @pl.loop(0, n // step_rows)
    def _(index):
        rows = pl.ds(pl.multiple_of(index * step_rows, step_rows), step_rows)
        away = (state[rows, :].astype(F32) - mean).astype(jnp.bfloat16)
        spread_out[rows, :] = away
        anomaly_ref[rows, :] = away[:, :here]

    high = mean.astype(jnp.bfloat16)
    rest = mean - high.astype(F32)
    middle = rest.astype(jnp.bfloat16)
    small = (rest - middle.astype(F32)).astype(jnp.bfloat16)
    spread_out[n:, :] = jnp.concatenate([high, middle, small, jnp.zeros((13, wide), jnp.bfloat16)], axis=0)
    projected = jnp.dot(spread_out[...], table[...], preferred_element_type=F32)
    root = jnp.sqrt(precision_ref[...])
    observed = projected[n : n + 1] + (projected[n + 1 : n + 2] + projected[n + 2 : n + 3])
    innovation = (root * (reading_ref[...] - observed)).astype(jnp.bfloat16)
    weighted[:n, :] = (root * projected[:n]).astype(jnp.bfloat16)
    weighted[n:, :] = jnp.concatenate([innovation, jnp.zeros((15, innovation.shape[1]), jnp.bfloat16)], axis=0)

    a_piece = a_out.shape[1] - ROWS
    b_piece = b_out.shape[1]
    a_rows = n_mem * a_piece
    place = 0
    pull = []
    for begin in range(0, n, LANES):
        product = lax.dot_general(
            weighted[begin:, :], weighted[begin : begin + LANES, :], (((1,), (1,)), ((), ())), preferred_element_type=F32
        )
        pull.append(product[n - begin : n - begin + 1])
        for row in range(0, n - begin, ROWS):
            tile = product[row : row + ROWS]
            if place < a_rows:
                a_out[place // a_piece, place % a_piece : place % a_piece + ROWS, :] = tile
            else:
                spot = place - a_rows
                b_out[spot // b_piece, spot % b_piece : spot % b_piece + ROWS, :] = tile
            place += ROWS
    pull_tile = jnp.concatenate(pull + [jnp.zeros((ROWS - len(pull), LANES), F32)], axis=0)
    for s in range(n_mem):
        a_out[s, a_piece:, :] = pull_tile

    def begin_all(sources, target, peer, sems, count):
        copies = [
            pltpu.make_async_remote_copy(
                src_ref=sources(step), dst_ref=target(step), send_sem=sems.at[0, step - 1], recv_sem=sems.at[1, step - 1],
                device_id=peer(step), device_id_type=MESH,
            )
            for step in range(1, count)
        ]
        for copy in copies:
            copy.start()
        pending.extend(copies)
        return copies

    def arrived(copies):
        for copy in copies:
            copy.wait_recv()

    pending = []
    a_part = az.shape[1] - ROWS
    b_part = bz.shape[1]
    a1 = begin_all(lambda s: a_out.at[lax.rem(mem + s, n_mem)], lambda s: a_in.at[s - 1], mem_peer, a_sem, n_mem)
    b1 = begin_all(lambda s: b_out.at[lax.rem(y + s, n_y)], lambda s: b_in.at[s - 1], y_peer, b_sem, n_y)
    arrived(a1)
    summed = a_out[mem]
    for s in range(n_mem - 1):
        summed = summed + a_in[s]
    for s in range(n_y):
        ay_out[s, :a_part, :] = summed[s * a_part : (s + 1) * a_part]
        ay_out[s, a_part:, :] = summed[a_piece:]
    a2 = begin_all(lambda s: ay_out.at[lax.rem(y + s, n_y)], lambda s: ay_in.at[s - 1], y_peer, ay_sem, n_y)
    arrived(b1)
    summed = b_out[y]
    for s in range(n_y - 1):
        summed = summed + b_in[s]
    for s in range(n_mem):
        bm_out[s] = summed[s * b_part : (s + 1) * b_part]
    b2 = begin_all(lambda s: bm_out.at[lax.rem(mem + s, n_mem)], lambda s: bm_in.at[s - 1], mem_peer, bm_sem, n_mem)
    arrived(a2)
    summed = ay_out[y]
    for s in range(n_y - 1):
        summed = summed + ay_in[s]
    az[z] = summed
    a3 = begin_all(lambda s: az.at[z], lambda s: az.at[z], z_peer, az_sem, n_z)
    arrived(b2)
    summed = bm_out[mem]
    for s in range(n_mem - 1):
        summed = summed + bm_in[s]
    bz[z] = summed
    b3 = begin_all(lambda s: bz.at[z], lambda s: bz.at[z], z_peer, bz_sem, n_z)
    arrived(a3)
    summed = az[0]
    for s in range(1, n_z):
        summed = summed + az[s]
    pulled_ref[...] = summed[a_part:]
    a_slab = pl.ds(pl.multiple_of(mem * a_piece, a_piece), a_piece)
    a_own = pl.ds(pl.multiple_of(mem * a_piece + y * a_part, ROWS), a_part)
    total_ref[a_own, :] = summed[:a_part]
    a4 = begin_all(lambda s: total_ref.at[a_own], lambda s: total_ref.at[a_own], y_peer, ag_sem, n_y)
    arrived(b3)
    summed = bz[0]
    for s in range(1, n_z):
        summed = summed + bz[s]
    b_slab = pl.ds(pl.multiple_of(a_rows + y * b_piece, ROWS), b_piece)
    b_own = pl.ds(pl.multiple_of(a_rows + y * b_piece + mem * b_part, ROWS), b_part)
    total_ref[b_own, :] = summed
    b4 = begin_all(lambda s: total_ref.at[b_own], lambda s: total_ref.at[b_own], mem_peer, bg_sem, n_mem)
    arrived(a4)
    a5 = begin_all(lambda s: total_ref.at[a_slab], lambda s: total_ref.at[a_slab], mem_peer, ah_sem, n_mem)
    arrived(b4)
    b5 = begin_all(lambda s: total_ref.at[b_slab], lambda s: total_ref.at[b_slab], y_peer, bh_sem, n_y)
    arrived(a5)
    arrived(b5)
    for copy in pending:
        copy.wait_send()
    edge_copy(mem).wait_send()
    for step in range(1, n_mem):
        target = lax.rem(mem + step, n_mem)

        @pl.when(target != last)
        def _(step=step):
            slab_copy(step, wide).wait_send()

        @pl.when(target == last)
        def _(step=step):
            slab_copy(step, here).wait_send()


def front(field, start, weights, readings, precision, n_y, n_z):
    members, slab = field.shape
    n_mem = lax.axis_size("mem")
    n, here = members * n_mem, slab // n_mem
    observations = start.shape[1]
    blocks = n // LANES
    packed = LANES * blocks * (blocks + 1) // 2
    a_part = packed * 3 // 5 // (n_mem * n_y)
    b_part = (packed - a_part * n_mem * n_y) // (n_mem * n_y)
    a_piece, b_piece = a_part * n_y, b_part * n_mem
    dma = pltpu.SemaphoreType.DMA
    vmem = pl.BlockSpec(memory_space=pltpu.VMEM)
    bf16 = jnp.bfloat16
    return pl.pallas_call(
        functools.partial(front_kernel, n_mem, n_y, n_z),
        out_shape=(
            jax.ShapeDtypeStruct((packed, LANES), F32),
            jax.ShapeDtypeStruct((ROWS, LANES), F32),
            jax.ShapeDtypeStruct((n, here), bf16),
            jax.ShapeDtypeStruct((1, here), F32),
        ),
        in_specs=[pl.BlockSpec(memory_space=pl.ANY)] + [vmem] * 4,
        out_specs=(vmem,) * 4,
        scratch_shapes=[
            pltpu.VMEM((n, here + LANES), bf16),
            pltpu.VMEM((n + 16, here + LANES), bf16),
            pltpu.VMEM((here + LANES, observations), bf16),
            pltpu.VMEM((n + 16, observations), bf16),
            pltpu.VMEM((n_mem, a_piece + ROWS, LANES), F32),
            pltpu.VMEM((n_mem - 1, a_piece + ROWS, LANES), F32),
            pltpu.VMEM((n_y, b_piece, LANES), F32),
            pltpu.VMEM((n_y - 1, b_piece, LANES), F32),
            pltpu.VMEM((n_y, a_part + ROWS, LANES), F32),
            pltpu.VMEM((n_y - 1, a_part + ROWS, LANES), F32),
            pltpu.VMEM((n_mem, b_part, LANES), F32),
            pltpu.VMEM((n_mem - 1, b_part, LANES), F32),
            pltpu.VMEM((n_z, a_part + ROWS, LANES), F32),
            pltpu.VMEM((n_z, b_part, LANES), F32),
            dma, dma, dma((n_mem,)), dma((n_mem - 1,)), dma((n_mem - 1,)),
            dma((2, n_mem - 1)), dma((2, n_y - 1)), dma((2, n_y - 1)), dma((2, n_mem - 1)),
            dma((2, n_z - 1)), dma((2, n_z - 1)),
            dma((2, n_y - 1)), dma((2, n_mem - 1)), dma((2, n_mem - 1)), dma((2, n_y - 1)),
        ],
        compiler_params=pltpu.CompilerParams(collective_id=0, has_side_effects=True, vmem_limit_bytes=20 << 20),
        name="front",
    )(field, start, weights, readings, precision)

def precise_dot(left, right, contract=((1,), (0,))):
    return lax.dot_general(
        left, right, (contract, ((), ())), precision=lax.Precision.HIGHEST, preferred_element_type=F32
    )


def inverse_factor_rows(tiles, group):
    tiles = list(tiles)
    extent = tiles[0].shape[1]
    lane = lax.broadcasted_iota(jnp.int32, (ROWS, extent), 1)
    sublane = lax.broadcasted_iota(jnp.int32, (ROWS, extent), 0)

    def spread(value):
        return jnp.broadcast_to(value, (ROWS, extent))

    for first in range(0, extent, group):
        home, top = first // ROWS, first % ROWS
        own = tiles[home]
        columns = [
            [spread(tile[:, first + a : first + a + 1]) for tile in tiles[home:]] for a in range(group)
        ]
        pivots = {
            (b, a): spread(columns[a][0][top + b : top + b + 1, :]) for a in range(group) for b in range(a, group)
        }
        member = (lane >= first) & (lane < first + group)
        rows = [
            jnp.where(member, jnp.where(lane == first + a, 1.0, 0.0), spread(own[top + a : top + a + 1, :]))
            for a in range(group)
        ]
        for a in range(group):
            scale = lax.rsqrt(pivots[(a, a)])
            rows[a] = rows[a] * scale
            columns[a] = [column * scale for column in columns[a]]
            below = {b: pivots[(b, a)] * scale for b in range(a + 1, group)}
            for b in range(a + 1, group):
                for c in range(a + 1, b + 1):
                    pivots[(b, c)] = pivots[(b, c)] - below[b] * below[c]
                rows[b] = rows[b] - below[b] * rows[a]
                columns[b] = [right - left * below[b] for right, left in zip(columns[b], columns[a])]
        for index in range(home, len(tiles)):
            if index == home and group == ROWS:
                fresh = own
            else:
                fresh = jnp.where(member, 0.0, tiles[index])
                for a in range(group):
                    fresh = fresh - columns[a][index - home] * rows[a]
            if index == home:
                fresh = jnp.where(sublane < top, own, fresh)
                for a in range(group):
                    fresh = jnp.where(sublane == top + a, rows[a], fresh)
            tiles[index] = fresh
    return tiles


def mixing_kernel(n, width, group, packed_ref, pull_ref, out_ref, work):
    shape = (width, width)
    row = lax.broadcasted_iota(jnp.int32, shape, 0)
    column = lax.broadcasted_iota(jnp.int32, shape, 1)
    unit = jnp.where(row == column, 1.0, 0.0)
    place = 0
    for begin in range(0, n, width):
        work[begin:n, begin : begin + width] = packed_ref[place : place + n - begin, :]
        place += n - begin
        index = begin // width
        work[n : n + 1, begin : begin + width] = pull_ref[index : index + 1, :]
    work[n + 1 :, :] = jnp.zeros((ROWS - 1, n), F32)
    for begin in range(0, n, width):
        end = begin + width
        block = work[begin:end, begin:end] + (n - 1.0) * unit
        tiles = inverse_factor_rows([block[i : i + ROWS] for i in range(0, width, ROWS)], group)
        inverse = jnp.where(column <= row, jnp.concatenate(tiles, axis=0), 0.0)
        below = precise_dot(work[end:, begin:end], inverse, ((1,), (1,)))
        if begin > 0:
            work[begin:end, :begin] = precise_dot(inverse, work[begin:end, :begin])
        work[begin:end, begin:end] = inverse
        work[end:, begin:end] = jnp.zeros((n + ROWS - end, width), F32)
        work[end:, :end] = work[end:, :end] - precise_dot(below, work[begin:end, :end])
        if end < n:
            work[end:, end:] = work[end:, end:] - precise_dot(below, below[: n - end], ((1,), (1,)))
    whole = (n, n)
    lower = lax.broadcasted_iota(jnp.int32, whole, 1) <= lax.broadcasted_iota(jnp.int32, whole, 0)
    scaled = jnp.where(lower, work[:n, :] * math.sqrt(n - 1.0), 0.0)
    out_ref[...] = (scaled - work[n : n + 1, :]).astype(jnp.bfloat16)


def mixing_rows(packed, pull_tile, n):
    return pl.pallas_call(
        functools.partial(mixing_kernel, n, LANES, ROWS),
        out_shape=jax.ShapeDtypeStruct((n, n), jnp.bfloat16),
        in_specs=[pl.BlockSpec(memory_space=pltpu.VMEM)] * 2,
        out_specs=pl.BlockSpec(memory_space=pltpu.VMEM),
        scratch_shapes=[pltpu.VMEM((n + ROWS, n), F32)],
        compiler_params=pltpu.CompilerParams(vmem_limit_bytes=24 << 20),
        name="mixing",
    )(packed, pull_tile)


def local(
    background_copies,
    measuring_span_leading_cell,
    measuring_kernel_coefficients,
    measured_readings,
    measured_error_precision,
):
    predicted_copies = background_copies.shape[0] * lax.axis_size("mem")
    total, pulled, copy_anomalies, predicted_centroid = front(
        background_copies,
        measuring_span_leading_cell[None, :],
        jnp.transpose(measuring_kernel_coefficients),
        measured_readings[None, :],
        measured_error_precision[None, :],
        N_Y,
        lax.axis_size("cells") // N_Y,
    )
    mixing_transposed = mixing_rows(total, pulled, predicted_copies)
    return predicted_centroid + lax.dot_general(
        mixing_transposed, copy_anomalies, (((1,), (0,)), ((), ())), preferred_element_type=jnp.float32
    )


def solution(mesh):
    in_specs = (
        P("mem", "cells"),
        P(("cells", "mem")),
        P(("cells", "mem"), None),
        P(("cells", "mem")),
        P(("cells", "mem")),
    )
    out_specs = P(None, ("cells", "mem"))
    return jax.shard_map(local, mesh=mesh, in_specs=in_specs, out_specs=out_specs, check_vma=False)
```

time: 105 us -> 82 us (0.78)
  waiting for transfers between devices: 15.1 us -> 0 us
  Pallas kernels: 67.5 us -> 75.8 us
  starting transfers between devices: 7.65 us -> 0 us
  matrix products: 9.36 us -> 2.03 us
    all_to_all x1 -> x0, waiting for transfers between devices: 15.1 us -> none  [local(): lax.all_to_all(background_copies, 'mem', split_axis=1, concat_axis=0, til...]
    pallas_call x1, Pallas kernels: 44.1 us -> 52.4 us  [front(): pl.pallas_call(functools.partial(front_kernel, n_mem, n_y, n_z), out_shap...]
    dot_general x6 -> x0, matrix products: 7.31 us -> none  [the longest x1 2.03 us: local(): jnp.dot(primary_lookup.astype(jnp.float32), predicted_centroid, precision...]
    all_to_all x1 -> x0, starting transfers between devices: 6.7 us -> none  [local(): lax.all_to_all(background_copies, 'mem', split_axis=1, concat_axis=0, til...]
    all_to_all x1 -> x0, local copies, waits for them, and re-layouts: 2.31 us -> none  [local(): lax.all_to_all(background_copies, 'mem', split_axis=1, concat_axis=0, til...]
    unnamed x12 -> x10, local copies, waits for them, and re-layouts: 1.81 us -> 3.95 us
  transfers between devices with their start and end apart: 2 -> 0, of which waited for: 1 -> 0; matrix products, arithmetic and copies ran while one was open for 3% -> 0% of each run, Pallas kernels for 0% -> 0%
where the time goes in v2:
time: 82 us; the launch traced here: 81.8 us
  Pallas kernels  75.8 us (92%)
  local copies, waits for them, and re-layouts  3.95 us (5%)
  matrix products  2.03 us (2%)
    pallas_call x1, Pallas kernels, front(): pl.pallas_call(functools.partial(front_kernel, n_mem, n_y, n_z), out_shap...  52.4 us
    pallas_call x1, Pallas kernels, mixing_rows(): pl.pallas_call(functools.partial(mixing_kernel, n, LANES, ROWS), out_shap...  23.3 us
    unnamed x10, local copies, waits for them, and re-layouts  3.95 us
    dot_general x1, matrix products, local(): lax.dot_general(mixing_transposed, copy_anomalies, (((1,), (0,)), ((), ()...  2.03 us

profile of v2, /device:TPU:1, one launch (start us, length us, event | category | flops | bytes accessed | tf_op | source)
XLA Modules:
  0.0 81.8 jit_solution(7070444987839840374)
XLA Ops:
  0.0 0.0 copy-start
  0.0 1.2 %copy-done = bf16[64,8192]{1,0:T(8,128)(2,1)S(1)} copy-done((bf16[64,8192]{1,0:T(8,128)(2,1)S(1)}, bf16[64,8192]{1,0:T(8,128)(2,1)}, u32[]{:S(2)}) %copy-start) | copy-done | bytes 1048600
  1.2 0.0 copy-start.1
  1.2 0.7 copy-done.1
  1.9 0.0 copy-start.2
  1.9 0.7 copy-done.2
  2.6 0.0 copy-start.3
  2.6 0.7 copy-done.3
  3.3 0.0 copy-start.4
  3.3 0.7 copy-done.4
  4.0 52.4 %front.1 = (f32[1280,128]{1,0:T(8,128)S(1)}, f32[8,128]{1,0:T(8,128)S(1)}, bf16[512,1024]{1,0:T(8,128)(2,1)S(1)}, f32[1,1024]{1,0:T(1,128)S(1)}) custom-call(bf16[64,8192]{1,0:T(8,128)(2,1)S(1)} %copy-done, s32[1,512]{1,0:T(1,128)S(1)} %bitcast.8, bf16[4,512]{1,0:T(4,128)(2,1)S(1)} %bitcast.7, f32[1,512]{1,0:T(1,128)S(1)} %bitcast.9, f32[1,512]{1,0:T(1,128)S(1)} %bitcast.10), custom_call_target="tpu_custom_call" | custom-call | tf_op jit(solution)/shard_map/front/pallas_call | solution.py:292
  56.4 23.3 %mixing.1 = bf16[512,512]{1,0:T(8,128)(2,1)S(1)} custom-call(f32[1280,128]{1,0:T(8,128)S(1)} %get-tuple-element.10.packed_ref, f32[8,128]{1,0:T(8,128)S(1)} %get-tuple-element.11.pull_ref), custom_call_target="tpu_custom_call" | custom-call | tf_op jit(solution)/shard_map/mixing/pallas_call | solution.py:412
  79.7 2.0 %convolution_add_fusion = f32[512,1024]{1,0:T(8,128)} fusion(bf16[512,512]{1,0:T(8,128)(2,1)S(1)} %mixing.1, bf16[512,1024]{1,0:T(8,128)(2,1)S(1)} %get-tuple-element.12, f32[1024]{0:T(1024)S(1)} %bitcast.11), kind=kOutput, calls=%fused_computation | convolution fusion | flops 537395200 | bytes 3674112 | tf_op jit(solution)/shard_map/dot_general | solution.py:441
Async XLA Ops:
  0.0 1.2 %copy-start = (bf16[64,8192]{1,0:T(8,128)(2,1)S(1)}, bf16[64,8192]{1,0:T(8,128)(2,1)}, u32[]{:S(2)}) copy-start(bf16[64,8192]{1,0:T(8,128)(2,1)} %field_ref.1) | copy-start | bytes 3145732
  1.2 0.7 copy-start.1
  1.9 0.7 copy-start.2
  2.6 0.7 copy-start.3
  3.3 0.7 copy-start.4

commit v3 on v2

--- a/solution.py
+++ b/solution.py
@@ -14,10 +14,10 @@
 MESH = pl.DeviceIdType.MESH
 
 
-def front_kernel(n_mem, n_y, n_z, field_ref, start_ref, weight_ref, reading_ref, precision_ref,
+def front_kernel(n_mem, n_y, n_z, field_ref, start_hbm, weight_hbm, reading_hbm, precision_hbm,
                  total_ref, pulled_ref, anomaly_ref, mean_ref,
-                 state, spread_out, table, weighted, a_out, a_in, b_out, b_in, ay_out, ay_in, bm_out, bm_in, az, bz,
-                 own_sem, edge_send, edge_recv, x_send, x_recv,
+                 start_ref, weight_ref, reading_ref, precision_ref, state, spread_out, table, weighted, a_out, a_in, b_out, b_in, ay_out, ay_in, bm_out, bm_in, az, bz,
+                 small_sem, own_sem, edge_send, edge_recv, x_send, x_recv,
                  a_sem, b_sem, ay_sem, bm_sem, az_sem, bz_sem, ag_sem, bg_sem, ah_sem, bh_sem):
     cell, mem = lax.axis_index("cells"), lax.axis_index("mem")
     n_cells = n_y * n_z
@@ -41,6 +41,15 @@
     def signal(peer):
         pl.semaphore_signal(barrier, inc=1, device_id=peer, device_id_type=MESH)
 
+    small = [
+        pltpu.make_async_copy(source, target, small_sem.at[index])
+        for index, (source, target) in enumerate(
+            ((start_hbm, start_ref), (weight_hbm, weight_ref), (reading_hbm, reading_ref), (precision_hbm, precision_ref))
+        )
+    ]
+    for copy in small:
+        copy.start()
+
     barrier = pltpu.get_barrier_semaphore()
     for step in range(1, n_mem):
         signal(mem_peer(step))
@@ -54,9 +63,23 @@
         for source in range(n_mem):
             signal((lax.rem(cell + 1, n_cells), source))
 
+    rows_here = pl.ds(pl.multiple_of(mem * members, members), members)
+
+    def own_copy(width):
+        return pltpu.make_async_copy(
+            field_ref.at[:, pl.ds(pl.multiple_of(mem * here, here), width)],
+            state.at[rows_here, pl.ds(0, width)], own_sem,
+        )
+
+    @pl.when(mem != last)
+    def _():
+        own_copy(wide).start()
+
+    @pl.when(mem == last)
+    def _():
+        own_copy(here).start()
+
     pl.semaphore_wait(barrier, n_mem + n_y + n_z - 2)
-
-    rows_here = pl.ds(pl.multiple_of(mem * members, members), members)
 
     def slab_copy(step, width):
         target = lax.rem(mem + step, n_mem)
@@ -76,12 +99,6 @@
             device_id=mem_peer(step), device_id_type=MESH,
         )
 
-    def own_copy(width):
-        return pltpu.make_async_copy(
-            field_ref.at[:, pl.ds(pl.multiple_of(mem * here, here), width)],
-            state.at[rows_here, pl.ds(0, width)], own_sem,
-        )
-
     def edge_copy(source):
         rows = pl.ds(pl.multiple_of(source * members, members), members)
         return pltpu.make_async_remote_copy(
@@ -103,14 +120,8 @@
 
     edge_copy(mem).start()
 
-    @pl.when(mem != last)
-    def _():
-        own_copy(wide).start()
-
-    @pl.when(mem == last)
-    def _():
-        own_copy(here).start()
-
+    for copy in small:
+        copy.wait()
     start = start_ref[...]
     taps = [weight_ref[j : j + 1, :].astype(F32) for j in range(weight_ref.shape[0])]
     chunk = 64
@@ -297,9 +308,13 @@
             jax.ShapeDtypeStruct((n, here), bf16),
             jax.ShapeDtypeStruct((1, here), F32),
         ),
-        in_specs=[pl.BlockSpec(memory_space=pl.ANY)] + [vmem] * 4,
+        in_specs=[pl.BlockSpec(memory_space=pltpu.HBM)] * 5,
         out_specs=(vmem,) * 4,
         scratch_shapes=[
+            pltpu.VMEM(start.shape, start.dtype),
+            pltpu.VMEM(weights.shape, weights.dtype),
+            pltpu.VMEM(readings.shape, readings.dtype),
+            pltpu.VMEM(precision.shape, precision.dtype),
             pltpu.VMEM((n, here + LANES), bf16),
             pltpu.VMEM((n + 16, here + LANES), bf16),
             pltpu.VMEM((here + LANES, observations), bf16),
@@ -314,14 +329,14 @@
             pltpu.VMEM((n_mem - 1, b_part, LANES), F32),
             pltpu.VMEM((n_z, a_part + ROWS, LANES), F32),
             pltpu.VMEM((n_z, b_part, LANES), F32),
-            dma, dma, dma((n_mem,)), dma((n_mem - 1,)), dma((n_mem - 1,)),
+            dma((4,)), dma, dma, dma((n_mem,)), dma((n_mem - 1,)), dma((n_mem - 1,)),
             dma((2, n_mem - 1)), dma((2, n_y - 1)), dma((2, n_y - 1)), dma((2, n_mem - 1)),
             dma((2, n_z - 1)), dma((2, n_z - 1)),
             dma((2, n_y - 1)), dma((2, n_mem - 1)), dma((2, n_mem - 1)), dma((2, n_y - 1)),
         ],
         compiler_params=pltpu.CompilerParams(collective_id=0, has_side_effects=True, vmem_limit_bytes=20 << 20),
         name="front",
-    )(field, start, weights, readings, precision)
+    )(*(pltpu.with_memory_space_constraint(x, pltpu.HBM) for x in (field, start, weights, readings, precision)))
 
 def precise_dot(left, right, contract=((1,), (0,))):
     return lax.dot_general(
@@ -329,8 +344,9 @@
     )
 
 
-def inverse_factor_rows(tiles, group):
+def inverse_factor_rows(tiles, panel, ahead):
     tiles = list(tiles)
+    count = len(tiles)
     extent = tiles[0].shape[1]
     lane = lax.broadcasted_iota(jnp.int32, (ROWS, extent), 1)
     sublane = lax.broadcasted_iota(jnp.int32, (ROWS, extent), 0)
@@ -338,46 +354,61 @@
     def spread(value):
         return jnp.broadcast_to(value, (ROWS, extent))
 
-    for first in range(0, extent, group):
-        home, top = first // ROWS, first % ROWS
+    def pick(tile, position):
+        return jnp.take_along_axis(tile, jnp.full((ROWS, extent), position, jnp.int32), axis=1)
+
+    for home in range(count):
+        first = home * ROWS
+        panel_end = min((home // panel + 1) * panel, count)
+        near_end = min(panel_end + ahead, count)
         own = tiles[home]
-        columns = [
-            [spread(tile[:, first + a : first + a + 1]) for tile in tiles[home:]] for a in range(group)
+        lanes = [pick(own, first + a) for a in range(ROWS)]
+        pivots = {(b, a): spread(lanes[a][b : b + 1, :]) for a in range(ROWS) for b in range(a, ROWS)}
+        member = (lane >= first) & (lane < first + ROWS)
+        rows = [
+            jnp.where(member, jnp.where(lane == first + a, 1.0, 0.0), spread(own[a : a + 1, :])) for a in range(ROWS)
         ]
-        pivots = {
-            (b, a): spread(columns[a][0][top + b : top + b + 1, :]) for a in range(group) for b in range(a, group)
-        }
-        member = (lane >= first) & (lane < first + group)
-        rows = [
-            jnp.where(member, jnp.where(lane == first + a, 1.0, 0.0), spread(own[top + a : top + a + 1, :]))
-            for a in range(group)
-        ]
-        for a in range(group):
+        scales = []
+        for a in range(ROWS):
             scale = lax.rsqrt(pivots[(a, a)])
+            scales.append(scale)
             rows[a] = rows[a] * scale
-            columns[a] = [column * scale for column in columns[a]]
-            below = {b: pivots[(b, a)] * scale for b in range(a + 1, group)}
-            for b in range(a + 1, group):
+            for b in range(a + 1, ROWS):
+                pivots[(b, a)] = pivots[(b, a)] * scale
+            for b in range(a + 1, ROWS):
                 for c in range(a + 1, b + 1):
-                    pivots[(b, c)] = pivots[(b, c)] - below[b] * below[c]
-                rows[b] = rows[b] - below[b] * rows[a]
-                columns[b] = [right - left * below[b] for right, left in zip(columns[b], columns[a])]
-        for index in range(home, len(tiles)):
-            if index == home and group == ROWS:
-                fresh = own
-            else:
-                fresh = jnp.where(member, 0.0, tiles[index])
-                for a in range(group):
-                    fresh = fresh - columns[a][index - home] * rows[a]
-            if index == home:
-                fresh = jnp.where(sublane < top, own, fresh)
-                for a in range(group):
-                    fresh = jnp.where(sublane == top + a, rows[a], fresh)
+                    pivots[(b, c)] = pivots[(b, c)] - pivots[(b, a)] * pivots[(c, a)]
+                rows[b] = rows[b] - pivots[(b, a)] * rows[a]
+        fresh = rows[0]
+        for a in range(1, ROWS):
+            fresh = jnp.where(sublane == a, rows[a], fresh)
+        tiles[home] = fresh
+        solved = list(rows)
+        for a in range(ROWS - 1, -1, -1):
+            solved[a] = solved[a] * scales[a]
+            for b in range(a):
+                solved[b] = solved[b] - pivots[(a, b)] * solved[a]
+        for index in range(home + 1, near_end):
+            tile = tiles[index]
+            fresh = jnp.where(member, 0.0, tile)
+            for a in range(ROWS):
+                fresh = fresh - pick(tile, first + a) * solved[a]
             tiles[index] = fresh
+        if home + 1 == panel_end and near_end < count:
+            begin = (home // panel) * panel
+            done = tiles[begin:panel_end]
+            masked = [
+                jnp.where((lane >= (begin + i + 1) * ROWS) & (lane < panel_end * ROWS), 0.0, tile)
+                for i, tile in enumerate(done)
+            ]
+            change = precise_dot(jnp.concatenate(done, axis=0), jnp.concatenate(masked, axis=0), ((0,), (0,)))
+            inside = (lane >= begin * ROWS) & (lane < panel_end * ROWS)
+            for index in range(near_end, count):
+                tiles[index] = jnp.where(inside, 0.0, tiles[index]) - change[index * ROWS : (index + 1) * ROWS]
     return tiles
 
 
-def mixing_kernel(n, width, group, packed_ref, pull_ref, out_ref, work):
+def analysis_kernel(n, width, packed_ref, pull_ref, anomaly_ref, mean_ref, out_hbm, work, out, sems):
     shape = (width, width)
     row = lax.broadcasted_iota(jnp.int32, shape, 0)
     column = lax.broadcasted_iota(jnp.int32, shape, 1)
@@ -389,35 +420,60 @@
         index = begin // width
         work[n : n + 1, begin : begin + width] = pull_ref[index : index + 1, :]
     work[n + 1 :, :] = jnp.zeros((ROWS - 1, n), F32)
+    diagonal = work[:width, :width]
     for begin in range(0, n, width):
         end = begin + width
-        block = work[begin:end, begin:end] + (n - 1.0) * unit
-        tiles = inverse_factor_rows([block[i : i + ROWS] for i in range(0, width, ROWS)], group)
+        block = diagonal + (n - 1.0) * unit
+        tiles = inverse_factor_rows([block[i : i + ROWS] for i in range(0, width, ROWS)], 4, 1)
         inverse = jnp.where(column <= row, jnp.concatenate(tiles, axis=0), 0.0)
-        below = precise_dot(work[end:, begin:end], inverse, ((1,), (1,)))
+        if end < n:
+            near = precise_dot(work[end : end + width, begin:end], inverse, ((1,), (1,)))
+            diagonal = work[end : end + width, end : end + width] - precise_dot(near, near, ((1,), (1,)))
+            far = precise_dot(work[end + width :, begin:end], inverse, ((1,), (1,)))
+            below = jnp.concatenate([near, far], axis=0)
+        else:
+            below = precise_dot(work[end:, begin:end], inverse, ((1,), (1,)))
         if begin > 0:
             work[begin:end, :begin] = precise_dot(inverse, work[begin:end, :begin])
+            work[end:, :begin] = work[end:, :begin] - precise_dot(below, work[begin:end, :begin])
         work[begin:end, begin:end] = inverse
-        work[end:, begin:end] = jnp.zeros((n + ROWS - end, width), F32)
-        work[end:, :end] = work[end:, :end] - precise_dot(below, work[begin:end, :end])
-        if end < n:
-            work[end:, end:] = work[end:, end:] - precise_dot(below, below[: n - end], ((1,), (1,)))
-    whole = (n, n)
-    lower = lax.broadcasted_iota(jnp.int32, whole, 1) <= lax.broadcasted_iota(jnp.int32, whole, 0)
-    scaled = jnp.where(lower, work[:n, :] * math.sqrt(n - 1.0), 0.0)
-    out_ref[...] = (scaled - work[n : n + 1, :]).astype(jnp.bfloat16)
-
-
-def mixing_rows(packed, pull_tile, n):
+        work[end:, begin:end] = -precise_dot(below, inverse)
+        if end + width < n:
+            work[end + width :, end : end + width] = work[end + width :, end : end + width] - precise_dot(far, near, ((1,), (1,)))
+            work[end + width :, end + width :] = work[end + width :, end + width :] - precise_dot(
+                far, far[: n - end - width], ((1,), (1,))
+            )
+        elif end < n:
+            work[n:, end:] = work[n:, end:] - precise_dot(far, near, ((1,), (1,)))
+    shift = -work[n : n + 1, :]
+    copies = []
+    for begin in range(0, n, width):
+        rows = slice(begin, begin + width)
+        place = lax.broadcasted_iota(jnp.int32, (width, n), 0) + begin
+        lower = lax.broadcasted_iota(jnp.int32, (width, n), 1) <= place
+        mixing = (jnp.where(lower, work[rows, :] * math.sqrt(n - 1.0), 0.0) + shift).astype(jnp.bfloat16)
+        out[rows, :] = mean_ref[...] + jnp.dot(mixing, anomaly_ref[...], preferred_element_type=F32)
+        copies.append(pltpu.make_async_copy(out.at[rows], out_hbm.at[rows], sems.at[begin // width]))
+        copies[-1].start()
+    for copy in copies:
+        copy.wait()
+
+
+def analysis(packed, pull_tile, anomaly, mean):
+    n, here = anomaly.shape
     return pl.pallas_call(
-        functools.partial(mixing_kernel, n, LANES, ROWS),
-        out_shape=jax.ShapeDtypeStruct((n, n), jnp.bfloat16),
-        in_specs=[pl.BlockSpec(memory_space=pltpu.VMEM)] * 2,
-        out_specs=pl.BlockSpec(memory_space=pltpu.VMEM),
-        scratch_shapes=[pltpu.VMEM((n + ROWS, n), F32)],
+        functools.partial(analysis_kernel, n, LANES),
+        out_shape=jax.ShapeDtypeStruct((n, here), F32),
+        in_specs=[pl.BlockSpec(memory_space=pltpu.VMEM)] * 4,
+        out_specs=pl.BlockSpec(memory_space=pltpu.HBM),
+        scratch_shapes=[
+            pltpu.VMEM((n + ROWS, n), F32),
+            pltpu.VMEM((n, here), F32),
+            pltpu.SemaphoreType.DMA((n // LANES,)),
+        ],
         compiler_params=pltpu.CompilerParams(vmem_limit_bytes=24 << 20),
-        name="mixing",
-    )(packed, pull_tile)
+        name="analysis",
+    )(packed, pull_tile, anomaly, mean)
 
 
 def local(
@@ -427,7 +483,6 @@
     measured_readings,
     measured_error_precision,
 ):
-    predicted_copies = background_copies.shape[0] * lax.axis_size("mem")
     total, pulled, copy_anomalies, predicted_centroid = front(
         background_copies,
         measuring_span_leading_cell[None, :],
@@ -437,10 +492,7 @@
         N_Y,
         lax.axis_size("cells") // N_Y,
     )
-    mixing_transposed = mixing_rows(total, pulled, predicted_copies)
-    return predicted_centroid + lax.dot_general(
-        mixing_transposed, copy_anomalies, (((1,), (0,)), ((), ())), preferred_element_type=jnp.float32
-    )
+    return analysis(total, pulled, copy_anomalies, predicted_centroid)
 
 
 def solution(mesh):

time: 82 us -> 72.3 us (0.88)
  local copies, waits for them, and re-layouts: 3.95 us -> 0 us
  Pallas kernels: 75.8 us -> 72.2 us
  matrix products: 2.03 us -> 0 us
    pallas_call x1, Pallas kernels: 23.3 us -> 19.3 us  [analysis(): pl.pallas_call(functools.partial(analysis_kernel, n, LANES), out_shape=ja...]
    unnamed x10 -> x0, local copies, waits for them, and re-layouts: 3.95 us -> none
    dot_general x1 -> x0, matrix products: 2.03 us -> none  [local(): lax.dot_general(mixing_transposed, copy_anomalies, (((1,), (0,)), ((), ()...]
where the time goes in v3:
time: 72.3 us; the launch traced here: 72.2 us
  Pallas kernels  72.2 us (100%)
    pallas_call x1, Pallas kernels, front(): pl.pallas_call(functools.partial(front_kernel, n_mem, n_y, n_z), out_shap...  52.9 us
    pallas_call x1, Pallas kernels, analysis(): pl.pallas_call(functools.partial(analysis_kernel, n, LANES), out_shape=ja...  19.3 us

profile of v3, /device:TPU:1, one launch (start us, length us, event | category | flops | bytes accessed | tf_op | source)
XLA Modules:
  0.0 72.2 jit_solution(8277794480561503985)
XLA Ops:
  0.0 52.9 %front.1 = (f32[1280,128]{1,0:T(8,128)S(1)}, f32[8,128]{1,0:T(8,128)S(1)}, bf16[512,1024]{1,0:T(8,128)(2,1)S(1)}, f32[1,1024]{1,0:T(1,128)S(1)}) custom-call(bf16[64,8192]{1,0:T(8,128)(2,1)} %field_ref.1, s32[1,512]{1,0:T(1,128)} %bitcast.5, bf16[4,512]{1,0:T(4,128)(2,1)} %bitcast.4, f32[1,512]{1,0:T(1,128)} %bitcast.6, f32[1,512]{1,0:T(1,128)} %bitcast.7), custom_call_target="tpu_custom_call" | custom-call | tf_op jit(solution)/shard_map/front/pallas_call | solution.py:303
  52.9 19.3 %analysis.1 = f32[512,1024]{1,0:T(8,128)} custom-call(f32[1280,128]{1,0:T(8,128)S(1)} %get-tuple-element.9.packed_ref, f32[8,128]{1,0:T(8,128)S(1)} %get-tuple-element.10.pull_ref, bf16[512,1024]{1,0:T(8,128)(2,1)S(1)} %get-tuple-element.11.anomaly_ref, f32[1,1024]{1,0:T(1,128)S(1)} %get-tuple-element.12.mean_ref), custom_call_target="tpu_custom_call" | custom-call | tf_op jit(solution)/shard_map/analysis/pallas_call | solution.py:464

commit v4 on v3

--- a/solution.py
+++ b/solution.py
@@ -10,18 +10,22 @@
 
 F32 = jnp.float32
 N_Y = 4
+N_CORE = 2
 ROWS, LANES = 8, 128
 MESH = pl.DeviceIdType.MESH
 
 
 def front_kernel(n_mem, n_y, n_z, field_ref, start_hbm, weight_hbm, reading_hbm, precision_hbm,
                  total_ref, pulled_ref, anomaly_ref, mean_ref,
-                 start_ref, weight_ref, reading_ref, precision_ref, state, spread_out, table, weighted, a_out, a_in, b_out, b_in, ay_out, ay_in, bm_out, bm_in, az, bz,
+                 start_ref, weight_ref, reading_ref, precision_ref, state, spread_out, table, weighted, a_local, a_core, b_local, b_core,
+                 a_out, a_in, b_out, b_in, ay_out, ay_in, bx_out, bx_in, az, bz,
                  small_sem, own_sem, edge_send, edge_recv, x_send, x_recv,
-                 a_sem, b_sem, ay_sem, bm_sem, az_sem, bz_sem, ag_sem, bg_sem, ah_sem, bh_sem):
+                 core_sem, a_sem, b_sem, ay_sem, bx_sem, az_sem, bz_sem, ag_sem, bg_sem, ah_sem, bh_sem, pair_sem):
     cell, mem = lax.axis_index("cells"), lax.axis_index("mem")
     n_cells = n_y * n_z
     y, z = lax.rem(cell, n_y), cell // n_y
+    n_x = n_mem // N_CORE
+    x, core = mem // N_CORE, lax.rem(mem, N_CORE)
     members = field_ref.shape[0]
     n = members * n_mem
     here = anomaly_ref.shape[1]
@@ -31,6 +35,12 @@
 
     def mem_peer(step):
         return (cell, lax.rem(mem + step, n_mem))
+
+    def x_peer(step):
+        return (cell, lax.rem(x + step, n_x) * N_CORE + core)
+
+    def core_peer(step):
+        return (cell, x * N_CORE + lax.rem(core + step, N_CORE))
 
     def y_peer(step):
         return (z * n_y + lax.rem(y + step, n_y), mem)
@@ -180,7 +190,8 @@
 
     a_piece = a_out.shape[1] - ROWS
     b_piece = b_out.shape[1]
-    a_rows = n_mem * a_piece
+    a_rows, b_rows = n_x * a_piece, n_y * b_piece
+    half = a_rows + b_rows
     place = 0
     pull = []
     for begin in range(0, n, LANES):
@@ -190,15 +201,17 @@
         pull.append(product[n - begin : n - begin + 1])
         for row in range(0, n - begin, ROWS):
             tile = product[row : row + ROWS]
-            if place < a_rows:
-                a_out[place // a_piece, place % a_piece : place % a_piece + ROWS, :] = tile
+            side, spot = place // half, place % half
+            if spot < a_rows:
+                a_local[side, spot // a_piece, spot % a_piece : spot % a_piece + ROWS, :] = tile
             else:
-                spot = place - a_rows
-                b_out[spot // b_piece, spot % b_piece : spot % b_piece + ROWS, :] = tile
+                spot -= a_rows
+                b_local[side, spot // b_piece, spot % b_piece : spot % b_piece + ROWS, :] = tile
             place += ROWS
     pull_tile = jnp.concatenate(pull + [jnp.zeros((ROWS - len(pull), LANES), F32)], axis=0)
-    for s in range(n_mem):
-        a_out[s, a_piece:, :] = pull_tile
+    for side in range(N_CORE):
+        for s in range(n_x):
+            a_local[side, s, a_piece:, :] = pull_tile
 
     def begin_all(sources, target, peer, sems, count):
         copies = [
@@ -220,11 +233,18 @@
     pending = []
     a_part = az.shape[1] - ROWS
     b_part = bz.shape[1]
-    a1 = begin_all(lambda s: a_out.at[lax.rem(mem + s, n_mem)], lambda s: a_in.at[s - 1], mem_peer, a_sem, n_mem)
+    other = lax.rem(core + 1, N_CORE)
+    a0 = begin_all(lambda s: a_local.at[other], lambda s: a_core, core_peer, core_sem.at[0], N_CORE)
+    b0 = begin_all(lambda s: b_local.at[other], lambda s: b_core, core_peer, core_sem.at[1], N_CORE)
+    arrived(a0)
+    a_out[...] = a_local[core] + a_core[...]
+    a1 = begin_all(lambda s: a_out.at[lax.rem(x + s, n_x)], lambda s: a_in.at[s - 1], x_peer, a_sem, n_x)
+    arrived(b0)
+    b_out[...] = b_local[core] + b_core[...]
     b1 = begin_all(lambda s: b_out.at[lax.rem(y + s, n_y)], lambda s: b_in.at[s - 1], y_peer, b_sem, n_y)
     arrived(a1)
-    summed = a_out[mem]
-    for s in range(n_mem - 1):
+    summed = a_out[x]
+    for s in range(n_x - 1):
         summed = summed + a_in[s]
     for s in range(n_y):
         ay_out[s, :a_part, :] = summed[s * a_part : (s + 1) * a_part]
@@ -234,9 +254,9 @@
     summed = b_out[y]
     for s in range(n_y - 1):
         summed = summed + b_in[s]
-    for s in range(n_mem):
-        bm_out[s] = summed[s * b_part : (s + 1) * b_part]
-    b2 = begin_all(lambda s: bm_out.at[lax.rem(mem + s, n_mem)], lambda s: bm_in.at[s - 1], mem_peer, bm_sem, n_mem)
+    for s in range(n_x):
+        bx_out[s] = summed[s * b_part : (s + 1) * b_part]
+    b2 = begin_all(lambda s: bx_out.at[lax.rem(x + s, n_x)], lambda s: bx_in.at[s - 1], x_peer, bx_sem, n_x)
     arrived(a2)
     summed = ay_out[y]
     for s in range(n_y - 1):
@@ -244,9 +264,9 @@
     az[z] = summed
     a3 = begin_all(lambda s: az.at[z], lambda s: az.at[z], z_peer, az_sem, n_z)
     arrived(b2)
-    summed = bm_out[mem]
-    for s in range(n_mem - 1):
-        summed = summed + bm_in[s]
+    summed = bx_out[x]
+    for s in range(n_x - 1):
+        summed = summed + bx_in[s]
     bz[z] = summed
     b3 = begin_all(lambda s: bz.at[z], lambda s: bz.at[z], z_peer, bz_sem, n_z)
     arrived(a3)
@@ -254,24 +274,31 @@
     for s in range(1, n_z):
         summed = summed + az[s]
     pulled_ref[...] = summed[a_part:]
-    a_slab = pl.ds(pl.multiple_of(mem * a_piece, a_piece), a_piece)
-    a_own = pl.ds(pl.multiple_of(mem * a_piece + y * a_part, ROWS), a_part)
+    base = core * half
+    a_slab = pl.ds(pl.multiple_of(base + x * a_piece, ROWS), a_piece)
+    a_own = pl.ds(pl.multiple_of(base + x * a_piece + y * a_part, ROWS), a_part)
     total_ref[a_own, :] = summed[:a_part]
     a4 = begin_all(lambda s: total_ref.at[a_own], lambda s: total_ref.at[a_own], y_peer, ag_sem, n_y)
     arrived(b3)
     summed = bz[0]
     for s in range(1, n_z):
         summed = summed + bz[s]
-    b_slab = pl.ds(pl.multiple_of(a_rows + y * b_piece, ROWS), b_piece)
-    b_own = pl.ds(pl.multiple_of(a_rows + y * b_piece + mem * b_part, ROWS), b_part)
+    b_slab = pl.ds(pl.multiple_of(base + a_rows + y * b_piece, ROWS), b_piece)
+    b_own = pl.ds(pl.multiple_of(base + a_rows + y * b_piece + x * b_part, ROWS), b_part)
     total_ref[b_own, :] = summed
-    b4 = begin_all(lambda s: total_ref.at[b_own], lambda s: total_ref.at[b_own], mem_peer, bg_sem, n_mem)
+    b4 = begin_all(lambda s: total_ref.at[b_own], lambda s: total_ref.at[b_own], x_peer, bg_sem, n_x)
     arrived(a4)
-    a5 = begin_all(lambda s: total_ref.at[a_slab], lambda s: total_ref.at[a_slab], mem_peer, ah_sem, n_mem)
+    a5 = begin_all(lambda s: total_ref.at[a_slab], lambda s: total_ref.at[a_slab], x_peer, ah_sem, n_x)
     arrived(b4)
     b5 = begin_all(lambda s: total_ref.at[b_slab], lambda s: total_ref.at[b_slab], y_peer, bh_sem, n_y)
+    a_all = pl.ds(pl.multiple_of(base, ROWS), a_rows)
+    b_all = pl.ds(pl.multiple_of(base + a_rows, ROWS), b_rows)
     arrived(a5)
+    a6 = begin_all(lambda s: total_ref.at[a_all], lambda s: total_ref.at[a_all], core_peer, pair_sem.at[0], N_CORE)
     arrived(b5)
+    b6 = begin_all(lambda s: total_ref.at[b_all], lambda s: total_ref.at[b_all], core_peer, pair_sem.at[1], N_CORE)
+    arrived(a6)
+    arrived(b6)
     for copy in pending:
         copy.wait_send()
     edge_copy(mem).wait_send()
@@ -294,9 +321,10 @@
     observations = start.shape[1]
     blocks = n // LANES
     packed = LANES * blocks * (blocks + 1) // 2
+    n_x = n_mem // N_CORE
     a_part = packed * 3 // 5 // (n_mem * n_y)
     b_part = (packed - a_part * n_mem * n_y) // (n_mem * n_y)
-    a_piece, b_piece = a_part * n_y, b_part * n_mem
+    a_piece, b_piece = a_part * n_y, b_part * n_x
     dma = pltpu.SemaphoreType.DMA
     vmem = pl.BlockSpec(memory_space=pltpu.VMEM)
     bf16 = jnp.bfloat16
@@ -319,20 +347,26 @@
             pltpu.VMEM((n + 16, here + LANES), bf16),
             pltpu.VMEM((here + LANES, observations), bf16),
             pltpu.VMEM((n + 16, observations), bf16),
-            pltpu.VMEM((n_mem, a_piece + ROWS, LANES), F32),
-            pltpu.VMEM((n_mem - 1, a_piece + ROWS, LANES), F32),
+            pltpu.VMEM((N_CORE, n_x, a_piece + ROWS, LANES), F32),
+            pltpu.VMEM((n_x, a_piece + ROWS, LANES), F32),
+            pltpu.VMEM((N_CORE, n_y, b_piece, LANES), F32),
+            pltpu.VMEM((n_y, b_piece, LANES), F32),
+            pltpu.VMEM((n_x, a_piece + ROWS, LANES), F32),
+            pltpu.VMEM((n_x - 1, a_piece + ROWS, LANES), F32),
             pltpu.VMEM((n_y, b_piece, LANES), F32),
             pltpu.VMEM((n_y - 1, b_piece, LANES), F32),
             pltpu.VMEM((n_y, a_part + ROWS, LANES), F32),
             pltpu.VMEM((n_y - 1, a_part + ROWS, LANES), F32),
-            pltpu.VMEM((n_mem, b_part, LANES), F32),
-            pltpu.VMEM((n_mem - 1, b_part, LANES), F32),
+            pltpu.VMEM((n_x, b_part, LANES), F32),
+            pltpu.VMEM((n_x - 1, b_part, LANES), F32),
             pltpu.VMEM((n_z, a_part + ROWS, LANES), F32),
             pltpu.VMEM((n_z, b_part, LANES), F32),
             dma((4,)), dma, dma, dma((n_mem,)), dma((n_mem - 1,)), dma((n_mem - 1,)),
-            dma((2, n_mem - 1)), dma((2, n_y - 1)), dma((2, n_y - 1)), dma((2, n_mem - 1)),
+            dma((2, 2, N_CORE - 1)),
+            dma((2, n_x - 1)), dma((2, n_y - 1)), dma((2, n_y - 1)), dma((2, n_x - 1)),
             dma((2, n_z - 1)), dma((2, n_z - 1)),
-            dma((2, n_y - 1)), dma((2, n_mem - 1)), dma((2, n_mem - 1)), dma((2, n_y - 1)),
+            dma((2, n_y - 1)), dma((2, n_x - 1)), dma((2, n_x - 1)), dma((2, n_y - 1)),
+            dma((2, 2, N_CORE - 1)),
         ],
         compiler_params=pltpu.CompilerParams(collective_id=0, has_side_effects=True, vmem_limit_bytes=20 << 20),
         name="front",
@@ -360,15 +394,20 @@
     for home in range(count):
         first = home * ROWS
         panel_end = min((home // panel + 1) * panel, count)
-        near_end = min(panel_end + ahead, count)
+        near_end = max(min(panel_end + ahead, count), min(home + 2, count))
         own = tiles[home]
-        lanes = [pick(own, first + a) for a in range(ROWS)]
+        lanes = later if home else [pick(own, first + a) for a in range(ROWS)]
         pivots = {(b, a): spread(lanes[a][b : b + 1, :]) for a in range(ROWS) for b in range(a, ROWS)}
         member = (lane >= first) & (lane < first + ROWS)
         rows = [
             jnp.where(member, jnp.where(lane == first + a, 1.0, 0.0), spread(own[a : a + 1, :])) for a in range(ROWS)
         ]
         scales = []
+        following = tiles[home + 1] if home + 1 < count else None
+        if following is not None:
+            columns = [pick(following, first + a) for a in range(ROWS)]
+            later = [pick(following, first + ROWS + c) for c in range(ROWS)]
+            following = jnp.where(member, 0.0, following)
         for a in range(ROWS):
             scale = lax.rsqrt(pivots[(a, a)])
             scales.append(scale)
@@ -379,6 +418,12 @@
                 for c in range(a + 1, b + 1):
                     pivots[(b, c)] = pivots[(b, c)] - pivots[(b, a)] * pivots[(c, a)]
                 rows[b] = rows[b] - pivots[(b, a)] * rows[a]
+            if following is not None:
+                columns[a] = columns[a] * scale
+                for b in range(a + 1, ROWS):
+                    columns[b] = columns[b] - columns[a] * pivots[(b, a)]
+                following = following - columns[a] * rows[a]
+                later = [part - columns[a] * spread(columns[a][c : c + 1, :]) for c, part in enumerate(later)]
         fresh = rows[0]
         for a in range(1, ROWS):
             fresh = jnp.where(sublane == a, rows[a], fresh)
@@ -388,7 +433,9 @@
             solved[a] = solved[a] * scales[a]
             for b in range(a):
                 solved[b] = solved[b] - pivots[(a, b)] * solved[a]
-        for index in range(home + 1, near_end):
+        if following is not None:
+            tiles[home + 1] = following
+        for index in range(home + 2, near_end):
             tile = tiles[index]
             fresh = jnp.where(member, 0.0, tile)
             for a in range(ROWS):

time: 72.3 us -> 68 us (0.941)
  Pallas kernels: 72.2 us -> 67.9 us
    pallas_call x1, Pallas kernels: 19.3 us -> 15.4 us  [analysis(): pl.pallas_call(functools.partial(analysis_kernel, n, LANES), out_shape=ja...]
where the time goes in v4:
time: 68 us; the launch traced here: 67.9 us
  Pallas kernels  67.9 us (100%)
    pallas_call x1, Pallas kernels, front(): pl.pallas_call(functools.partial(front_kernel, n_mem, n_y, n_z), out_shap...  52.5 us
    pallas_call x1, Pallas kernels, analysis(): pl.pallas_call(functools.partial(analysis_kernel, n, LANES), out_shape=ja...  15.4 us

profile of v4, /device:TPU:1, one launch (start us, length us, event | category | flops | bytes accessed | tf_op | source)
XLA Modules:
  0.0 67.9 jit_solution(12651364000648445417)
XLA Ops:
  0.0 52.5 %front.1 = (f32[1280,128]{1,0:T(8,128)S(1)}, f32[8,128]{1,0:T(8,128)S(1)}, bf16[512,1024]{1,0:T(8,128)(2,1)S(1)}, f32[1,1024]{1,0:T(1,128)S(1)}) custom-call(bf16[64,8192]{1,0:T(8,128)(2,1)} %field_ref.1, s32[1,512]{1,0:T(1,128)} %bitcast.5, bf16[4,512]{1,0:T(4,128)(2,1)} %bitcast.4, f32[1,512]{1,0:T(1,128)} %bitcast.6, f32[1,512]{1,0:T(1,128)} %bitcast.7), custom_call_target="tpu_custom_call" | custom-call | tf_op jit(solution)/shard_map/front/pallas_call | solution.py:331
  52.5 15.4 %analysis.1 = f32[512,1024]{1,0:T(8,128)} custom-call(f32[1280,128]{1,0:T(8,128)S(1)} %get-tuple-element.9.packed_ref, f32[8,128]{1,0:T(8,128)S(1)} %get-tuple-element.10.pull_ref, bf16[512,1024]{1,0:T(8,128)(2,1)S(1)} %get-tuple-element.11.anomaly_ref, f32[1,1024]{1,0:T(1,128)S(1)} %get-tuple-element.12.mean_ref), custom_call_target="tpu_custom_call" | custom-call | tf_op jit(solution)/shard_map/analysis/pallas_call | solution.py:511

commit v5 on v4

--- a/solution.py
+++ b/solution.py
@@ -17,10 +17,9 @@
 
 def front_kernel(n_mem, n_y, n_z, field_ref, start_hbm, weight_hbm, reading_hbm, precision_hbm,
                  total_ref, pulled_ref, anomaly_ref, mean_ref,
-                 start_ref, weight_ref, reading_ref, precision_ref, state, spread_out, table, weighted, a_local, a_core, b_local, b_core,
-                 a_out, a_in, b_out, b_in, ay_out, ay_in, bx_out, bx_in, az, bz,
+                 start_ref, weight_ref, reading_ref, precision_ref, state, spread_out, table, weighted, local_sums, core_in, plane_out, plane_in, z_in,
                  small_sem, own_sem, edge_send, edge_recv, x_send, x_recv,
-                 core_sem, a_sem, b_sem, ay_sem, bx_sem, az_sem, bz_sem, ag_sem, bg_sem, ah_sem, bh_sem, pair_sem):
+                 core_sem, plane_sem, z_sem, gather_sem, pair_sem):
     cell, mem = lax.axis_index("cells"), lax.axis_index("mem")
     n_cells = n_y * n_z
     y, z = lax.rem(cell, n_y), cell // n_y
@@ -36,14 +35,15 @@
     def mem_peer(step):
         return (cell, lax.rem(mem + step, n_mem))
 
-    def x_peer(step):
-        return (cell, lax.rem(x + step, n_x) * N_CORE + core)
+    n_plane = n_x * n_y
+    spot_here = x * n_y + y
+
+    def plane_peer(step):
+        spot = lax.rem(spot_here + step, n_plane)
+        return (z * n_y + lax.rem(spot, n_y), (spot // n_y) * N_CORE + core)
 
     def core_peer(step):
         return (cell, x * N_CORE + lax.rem(core + step, N_CORE))
-
-    def y_peer(step):
-        return (z * n_y + lax.rem(y + step, n_y), mem)
 
     def z_peer(step):
         return (lax.rem(z + step, n_z) * n_y + y, mem)
@@ -63,8 +63,8 @@
     barrier = pltpu.get_barrier_semaphore()
     for step in range(1, n_mem):
         signal(mem_peer(step))
-    for step in range(1, n_y):
-        signal(y_peer(step))
+    for step in range(1, n_plane):
+        signal(plane_peer(step))
     for step in range(1, n_z):
         signal(z_peer(step))
 
@@ -89,7 +89,7 @@
     def _():
         own_copy(here).start()
 
-    pl.semaphore_wait(barrier, n_mem + n_y + n_z - 2)
+    pl.semaphore_wait(barrier, n_mem + n_plane + n_z - 2)
 
     def slab_copy(step, width):
         target = lax.rem(mem + step, n_mem)
@@ -188,10 +188,8 @@
     weighted[:n, :] = (root * projected[:n]).astype(jnp.bfloat16)
     weighted[n:, :] = jnp.concatenate([innovation, jnp.zeros((15, innovation.shape[1]), jnp.bfloat16)], axis=0)
 
-    a_piece = a_out.shape[1] - ROWS
-    b_piece = b_out.shape[1]
-    a_rows, b_rows = n_x * a_piece, n_y * b_piece
-    half = a_rows + b_rows
+    part = plane_out.shape[1] - ROWS
+    half = n_plane * part
     place = 0
     pull = []
     for begin in range(0, n, LANES):
@@ -200,18 +198,13 @@
         )
         pull.append(product[n - begin : n - begin + 1])
         for row in range(0, n - begin, ROWS):
-            tile = product[row : row + ROWS]
             side, spot = place // half, place % half
-            if spot < a_rows:
-                a_local[side, spot // a_piece, spot % a_piece : spot % a_piece + ROWS, :] = tile
-            else:
-                spot -= a_rows
-                b_local[side, spot // b_piece, spot % b_piece : spot % b_piece + ROWS, :] = tile
+            local_sums[side, spot // part, spot % part : spot % part + ROWS, :] = product[row : row + ROWS]
             place += ROWS
     pull_tile = jnp.concatenate(pull + [jnp.zeros((ROWS - len(pull), LANES), F32)], axis=0)
     for side in range(N_CORE):
-        for s in range(n_x):
-            a_local[side, s, a_piece:, :] = pull_tile
+        for s in range(n_plane):
+            local_sums[side, s, part:, :] = pull_tile
 
     def begin_all(sources, target, peer, sems, count):
         copies = [
@@ -231,74 +224,29 @@
             copy.wait_recv()
 
     pending = []
-    a_part = az.shape[1] - ROWS
-    b_part = bz.shape[1]
     other = lax.rem(core + 1, N_CORE)
-    a0 = begin_all(lambda s: a_local.at[other], lambda s: a_core, core_peer, core_sem.at[0], N_CORE)
-    b0 = begin_all(lambda s: b_local.at[other], lambda s: b_core, core_peer, core_sem.at[1], N_CORE)
-    arrived(a0)
-    a_out[...] = a_local[core] + a_core[...]
-    a1 = begin_all(lambda s: a_out.at[lax.rem(x + s, n_x)], lambda s: a_in.at[s - 1], x_peer, a_sem, n_x)
-    arrived(b0)
-    b_out[...] = b_local[core] + b_core[...]
-    b1 = begin_all(lambda s: b_out.at[lax.rem(y + s, n_y)], lambda s: b_in.at[s - 1], y_peer, b_sem, n_y)
-    arrived(a1)
-    summed = a_out[x]
-    for s in range(n_x - 1):
-        summed = summed + a_in[s]
-    for s in range(n_y):
-        ay_out[s, :a_part, :] = summed[s * a_part : (s + 1) * a_part]
-        ay_out[s, a_part:, :] = summed[a_piece:]
-    a2 = begin_all(lambda s: ay_out.at[lax.rem(y + s, n_y)], lambda s: ay_in.at[s - 1], y_peer, ay_sem, n_y)
-    arrived(b1)
-    summed = b_out[y]
-    for s in range(n_y - 1):
-        summed = summed + b_in[s]
-    for s in range(n_x):
-        bx_out[s] = summed[s * b_part : (s + 1) * b_part]
-    b2 = begin_all(lambda s: bx_out.at[lax.rem(x + s, n_x)], lambda s: bx_in.at[s - 1], x_peer, bx_sem, n_x)
-    arrived(a2)
-    summed = ay_out[y]
-    for s in range(n_y - 1):
-        summed = summed + ay_in[s]
-    az[z] = summed
-    a3 = begin_all(lambda s: az.at[z], lambda s: az.at[z], z_peer, az_sem, n_z)
-    arrived(b2)
-    summed = bx_out[x]
-    for s in range(n_x - 1):
-        summed = summed + bx_in[s]
-    bz[z] = summed
-    b3 = begin_all(lambda s: bz.at[z], lambda s: bz.at[z], z_peer, bz_sem, n_z)
-    arrived(a3)
-    summed = az[0]
+    arrived(begin_all(lambda s: local_sums.at[other], lambda s: core_in, core_peer, core_sem, N_CORE))
+    plane_out[...] = local_sums[core] + core_in[...]
+    arrived(
+        begin_all(
+            lambda s: plane_out.at[lax.rem(spot_here + s, n_plane)], lambda s: plane_in.at[s - 1], plane_peer, plane_sem, n_plane
+        )
+    )
+    summed = plane_out[spot_here]
+    for s in range(n_plane - 1):
+        summed = summed + plane_in[s]
+    z_in[z] = summed
+    arrived(begin_all(lambda s: z_in.at[z], lambda s: z_in.at[z], z_peer, z_sem, n_z))
+    summed = z_in[0]
     for s in range(1, n_z):
-        summed = summed + az[s]
-    pulled_ref[...] = summed[a_part:]
+        summed = summed + z_in[s]
+    pulled_ref[...] = summed[part:]
     base = core * half
-    a_slab = pl.ds(pl.multiple_of(base + x * a_piece, ROWS), a_piece)
-    a_own = pl.ds(pl.multiple_of(base + x * a_piece + y * a_part, ROWS), a_part)
-    total_ref[a_own, :] = summed[:a_part]
-    a4 = begin_all(lambda s: total_ref.at[a_own], lambda s: total_ref.at[a_own], y_peer, ag_sem, n_y)
-    arrived(b3)
-    summed = bz[0]
-    for s in range(1, n_z):
-        summed = summed + bz[s]
-    b_slab = pl.ds(pl.multiple_of(base + a_rows + y * b_piece, ROWS), b_piece)
-    b_own = pl.ds(pl.multiple_of(base + a_rows + y * b_piece + x * b_part, ROWS), b_part)
-    total_ref[b_own, :] = summed
-    b4 = begin_all(lambda s: total_ref.at[b_own], lambda s: total_ref.at[b_own], x_peer, bg_sem, n_x)
-    arrived(a4)
-    a5 = begin_all(lambda s: total_ref.at[a_slab], lambda s: total_ref.at[a_slab], x_peer, ah_sem, n_x)
-    arrived(b4)
-    b5 = begin_all(lambda s: total_ref.at[b_slab], lambda s: total_ref.at[b_slab], y_peer, bh_sem, n_y)
-    a_all = pl.ds(pl.multiple_of(base, ROWS), a_rows)
-    b_all = pl.ds(pl.multiple_of(base + a_rows, ROWS), b_rows)
-    arrived(a5)
-    a6 = begin_all(lambda s: total_ref.at[a_all], lambda s: total_ref.at[a_all], core_peer, pair_sem.at[0], N_CORE)
-    arrived(b5)
-    b6 = begin_all(lambda s: total_ref.at[b_all], lambda s: total_ref.at[b_all], core_peer, pair_sem.at[1], N_CORE)
-    arrived(a6)
-    arrived(b6)
+    own = pl.ds(pl.multiple_of(base + spot_here * part, ROWS), part)
+    total_ref[own, :] = summed[:part]
+    arrived(begin_all(lambda s: total_ref.at[own], lambda s: total_ref.at[own], plane_peer, gather_sem, n_plane))
+    mine = pl.ds(pl.multiple_of(base, ROWS), half)
+    arrived(begin_all(lambda s: total_ref.at[mine], lambda s: total_ref.at[mine], core_peer, pair_sem, N_CORE))
     for copy in pending:
         copy.wait_send()
     edge_copy(mem).wait_send()
@@ -321,10 +269,8 @@
     observations = start.shape[1]
     blocks = n // LANES
     packed = LANES * blocks * (blocks + 1) // 2
-    n_x = n_mem // N_CORE
-    a_part = packed * 3 // 5 // (n_mem * n_y)
-    b_part = (packed - a_part * n_mem * n_y) // (n_mem * n_y)
-    a_piece, b_piece = a_part * n_y, b_part * n_x
+    n_plane = n_mem // N_CORE * n_y
+    part = packed // (N_CORE * n_plane)
     dma = pltpu.SemaphoreType.DMA
     vmem = pl.BlockSpec(memory_space=pltpu.VMEM)
     bf16 = jnp.bfloat16
@@ -347,26 +293,13 @@
             pltpu.VMEM((n + 16, here + LANES), bf16),
             pltpu.VMEM((here + LANES, observations), bf16),
             pltpu.VMEM((n + 16, observations), bf16),
-            pltpu.VMEM((N_CORE, n_x, a_piece + ROWS, LANES), F32),
-            pltpu.VMEM((n_x, a_piece + ROWS, LANES), F32),
-            pltpu.VMEM((N_CORE, n_y, b_piece, LANES), F32),
-            pltpu.VMEM((n_y, b_piece, LANES), F32),
-            pltpu.VMEM((n_x, a_piece + ROWS, LANES), F32),
-            pltpu.VMEM((n_x - 1, a_piece + ROWS, LANES), F32),
-            pltpu.VMEM((n_y, b_piece, LANES), F32),
-            pltpu.VMEM((n_y - 1, b_piece, LANES), F32),
-            pltpu.VMEM((n_y, a_part + ROWS, LANES), F32),
-            pltpu.VMEM((n_y - 1, a_part + ROWS, LANES), F32),
-            pltpu.VMEM((n_x, b_part, LANES), F32),
-            pltpu.VMEM((n_x - 1, b_part, LANES), F32),
-            pltpu.VMEM((n_z, a_part + ROWS, LANES), F32),
-            pltpu.VMEM((n_z, b_part, LANES), F32),
+            pltpu.VMEM((N_CORE, n_plane, part + ROWS, LANES), F32),
+            pltpu.VMEM((n_plane, part + ROWS, LANES), F32),
+            pltpu.VMEM((n_plane, part + ROWS, LANES), F32),
+            pltpu.VMEM((n_plane - 1, part + ROWS, LANES), F32),
+            pltpu.VMEM((n_z, part + ROWS, LANES), F32),
             dma((4,)), dma, dma, dma((n_mem,)), dma((n_mem - 1,)), dma((n_mem - 1,)),
-            dma((2, 2, N_CORE - 1)),
-            dma((2, n_x - 1)), dma((2, n_y - 1)), dma((2, n_y - 1)), dma((2, n_x - 1)),
-            dma((2, n_z - 1)), dma((2, n_z - 1)),
-            dma((2, n_y - 1)), dma((2, n_x - 1)), dma((2, n_x - 1)), dma((2, n_y - 1)),
-            dma((2, 2, N_CORE - 1)),
+            dma((2, N_CORE - 1)), dma((2, n_plane - 1)), dma((2, n_z - 1)), dma((2, n_plane - 1)), dma((2, N_CORE - 1)),
         ],
         compiler_params=pltpu.CompilerParams(collective_id=0, has_side_effects=True, vmem_limit_bytes=20 << 20),
         name="front",

time: 68 us -> 65.5 us (0.963)
  Pallas kernels: 67.9 us -> 65.4 us
    pallas_call x1, Pallas kernels: 52.5 us -> 50.1 us  [front(): pl.pallas_call(functools.partial(front_kernel, n_mem, n_y, n_z), out_shap...]
where the time goes in v5:
time: 65.5 us; the launch traced here: 65.4 us
  Pallas kernels  65.4 us (100%)
    pallas_call x1, Pallas kernels, front(): pl.pallas_call(functools.partial(front_kernel, n_mem, n_y, n_z), out_shap...  50.1 us
    pallas_call x1, Pallas kernels, analysis(): pl.pallas_call(functools.partial(analysis_kernel, n, LANES), out_shape=ja...  15.4 us

profile of v5, /device:TPU:1, one launch (start us, length us, event | category | flops | bytes accessed | tf_op | source)
XLA Modules:
  0.0 65.4 jit_solution(11575621325814507263)
XLA Ops:
  0.0 50.1 %front.1 = (f32[1280,128]{1,0:T(8,128)S(1)}, f32[8,128]{1,0:T(8,128)S(1)}, bf16[512,1024]{1,0:T(8,128)(2,1)S(1)}, f32[1,1024]{1,0:T(1,128)S(1)}) custom-call(bf16[64,8192]{1,0:T(8,128)(2,1)} %field_ref.1, s32[1,512]{1,0:T(1,128)} %bitcast.5, bf16[4,512]{1,0:T(4,128)(2,1)} %bitcast.4, f32[1,512]{1,0:T(1,128)} %bitcast.6, f32[1,512]{1,0:T(1,128)} %bitcast.7), custom_call_target="tpu_custom_call" | custom-call | tf_op jit(solution)/shard_map/front/pallas_call | solution.py:277
  50.1 15.4 %analysis.1 = f32[512,1024]{1,0:T(8,128)} custom-call(f32[1280,128]{1,0:T(8,128)S(1)} %get-tuple-element.9.packed_ref, f32[8,128]{1,0:T(8,128)S(1)} %get-tuple-element.10.pull_ref, bf16[512,1024]{1,0:T(8,128)(2,1)S(1)} %get-tuple-element.11.anomaly_ref, f32[1,1024]{1,0:T(1,128)S(1)} %get-tuple-element.12.mean_ref), custom_call_target="tpu_custom_call" | custom-call | tf_op jit(solution)/shard_map/analysis/pallas_call | solution.py:444

commit v6 on v5

--- a/solution.py
+++ b/solution.py
@@ -145,27 +145,35 @@
             block = jnp.where(ahead == j, tap, block)
         table[pl.ds(first, chunk), :] = block.astype(jnp.bfloat16)
 
+    step_rows = 64
+
+    def row_sums(source):
+        rows = pl.ds(pl.multiple_of(source * members, members), members)
+        return jnp.sum(state[rows, :].astype(F32).reshape(members // ROWS, ROWS, wide), axis=0)
+
     @pl.when(mem != last)
     def _():
         own_copy(wide).wait()
-        for step in range(1, n_mem):
-            arrival(step, wide).wait_recv()
 
     @pl.when(mem == last)
     def _():
         own_copy(here).wait()
-        for step in range(1, n_mem):
+        edge_copy(mem).wait_recv()
+
+    sums = row_sums(mem)
+    for step in range(1, n_mem):
+        source = lax.rem(mem + n_mem - step, n_mem)
+
+        @pl.when(mem != last)
+        def _(step=step):
+            arrival(step, wide).wait_recv()
+
+        @pl.when(mem == last)
+        def _(step=step, source=source):
             arrival(step, here).wait_recv()
-        for source in range(n_mem):
             edge_copy(source).wait_recv()
 
-    step_rows = 64
-
-    def add_rows(index, total):
-        first = pl.multiple_of(index * step_rows, step_rows)
-        return total + jnp.sum(state[pl.ds(first, step_rows), :].astype(F32).reshape(step_rows // ROWS, ROWS, wide), axis=0)
-
-    sums = lax.fori_loop(0, n // step_rows, add_rows, jnp.zeros((ROWS, wide), F32))
+        sums = sums + row_sums(source)
     mean = jnp.sum(sums, axis=0, keepdims=True) / n
     mean_ref[...] = mean[:, :here]
 
@@ -227,13 +235,12 @@
     other = lax.rem(core + 1, N_CORE)
     arrived(begin_all(lambda s: local_sums.at[other], lambda s: core_in, core_peer, core_sem, N_CORE))
     plane_out[...] = local_sums[core] + core_in[...]
-    arrived(
-        begin_all(
-            lambda s: plane_out.at[lax.rem(spot_here + s, n_plane)], lambda s: plane_in.at[s - 1], plane_peer, plane_sem, n_plane
-        )
+    shares = begin_all(
+        lambda s: plane_out.at[lax.rem(spot_here + s, n_plane)], lambda s: plane_in.at[s - 1], plane_peer, plane_sem, n_plane
     )
     summed = plane_out[spot_here]
-    for s in range(n_plane - 1):
+    for s, share in enumerate(shares):
+        share.wait_recv()
         summed = summed + plane_in[s]
     z_in[z] = summed
     arrived(begin_all(lambda s: z_in.at[z], lambda s: z_in.at[z], z_peer, z_sem, n_z))

time: 65.5 us -> 65.4 us (level)
  no operation moved by 1% of the time
where the time goes in v6:
time: 65.4 us; the launch traced here: 65.3 us
  Pallas kernels  65.3 us (100%)
    pallas_call x1, Pallas kernels, front(): pl.pallas_call(functools.partial(front_kernel, n_mem, n_y, n_z), out_shap...  49.9 us
    pallas_call x1, Pallas kernels, analysis(): pl.pallas_call(functools.partial(analysis_kernel, n, LANES), out_shape=ja...  15.4 us

profile of v6, /device:TPU:1, one launch (start us, length us, event | category | flops | bytes accessed | tf_op | source)
XLA Modules:
  0.0 65.3 jit_solution(13076232191369527715)
XLA Ops:
  0.0 49.9 %front.1 = (f32[1280,128]{1,0:T(8,128)S(1)}, f32[8,128]{1,0:T(8,128)S(1)}, bf16[512,1024]{1,0:T(8,128)(2,1)S(1)}, f32[1,1024]{1,0:T(1,128)S(1)}) custom-call(bf16[64,8192]{1,0:T(8,128)(2,1)} %field_ref.1, s32[1,512]{1,0:T(1,128)} %bitcast.5, bf16[4,512]{1,0:T(4,128)(2,1)} %bitcast.4, f32[1,512]{1,0:T(1,128)} %bitcast.6, f32[1,512]{1,0:T(1,128)} %bitcast.7), custom_call_target="tpu_custom_call" | custom-call | tf_op jit(solution)/shard_map/front/pallas_call | solution.py:284
  50.0 15.4 %analysis.1 = f32[512,1024]{1,0:T(8,128)} custom-call(f32[1280,128]{1,0:T(8,128)S(1)} %get-tuple-element.9.packed_ref, f32[8,128]{1,0:T(8,128)S(1)} %get-tuple-element.10.pull_ref, bf16[512,1024]{1,0:T(8,128)(2,1)S(1)} %get-tuple-element.11.anomaly_ref, f32[1,1024]{1,0:T(1,128)S(1)} %get-tuple-element.12.mean_ref), custom_call_target="tpu_custom_call" | custom-call | tf_op jit(solution)/shard_map/analysis/pallas_call | solution.py:451
